TPU v7x, 32 devices: a whole 2x2x4 slice. The times are simulated.
32 devices in a mesh: row: 8 (over y, x, core), col: 4 (over z).
Axes of the slice: x: 2, y: 2, z: 4, core: 2. Of those that a mesh axis runs over, the one named last changes fastest.
Arguments:
- panel_u: bfloat16 [2, 8, 1024, 160], P(None, 'row', 'col'), may hold values from -6 to 6
- panel_v: bfloat16 [2, 8, 1024, 160], P(None, 'row', 'col'), may hold values from -0.0625 to 0.0625
- panel_rank: int32 [2, 8], P(None, 'row'), may hold values from 32 to 160, as said below
- diag_inverse: bfloat16 [1024, 1024], P('col'), as said below
- tile_u: bfloat16 [2, 8, 4, 1024, 160], P(None, 'row', 'col'), may hold values from -6 to 6
- tile_v: bfloat16 [2, 8, 4, 1024, 160], P(None, 'row', 'col'), may hold values from -0.5 to 0.5
- tile_rank: int32 [2, 8, 4], P(None, 'row', 'col'), may hold values from 32 to 160, as said below
- sketch: bfloat16 [2, 8, 4, 1024, 160], P(None, 'row', 'col'), may hold values from -6 to 6
Outputs:
- new_u: float32 [2, 8, 4, 1024, 160], P(None, 'row', 'col')
- new_v: float32 [2, 8, 4, 1024, 160], P(None, 'row', 'col')
Inputs may be any that keep to these rules, and one draw needn't show every extreme that they name: `panel_rank`: some panel tile has rank 160. `tile_rank`: some trailing tile has rank 160. `diag_inverse`: lower triangular with diagonal entries of 1 to 2.
All inputs are finite; a program needn't handle non-finite values.
Results may differ from a plain program's by a relative error of at most 0.0037.
Values may be sent and summed in bfloat16 or wider, within the bound.
No kernel may reach another device: no remote copies, remote signals or barrier semaphores. Data moves between devices by JAX's collectives and lax.ppermute only.
A program may use at most 64 MiB of HBM per device.

v0:
```python
import functools
import math

import jax
import jax.numpy as jnp
from jax import lax
from jax.experimental import pallas as pl
from jax.experimental.pallas import tpu as pltpu
from jax.sharding import PartitionSpec as P


F32 = jnp.float32
BF16 = jnp.bfloat16
HIGH = lax.Precision.HIGHEST
GROUP = 8
SHARE_ROWS = 32
VMEM = pl.BlockSpec(memory_space=pltpu.VMEM)
SMEM = pl.BlockSpec(memory_space=pltpu.SMEM)
HBM = pl.BlockSpec(memory_space=pltpu.HBM)

NN = ((1,), (0,))
NT = ((1,), (1,))


def contract(a, b, dims, precision=None):
    return lax.dot_general(
        a, b, (dims, ((), ())), preferred_element_type=F32, precision=precision
    )


def stacked(value):
    head = value.astype(BF16)
    value = value - head.astype(F32)
    middle = value.astype(BF16)
    return jnp.concatenate([head, middle, (value - middle.astype(F32)).astype(BF16)], axis=0)


def folded(value):
    size = value.shape[0] // 3
    return value[:size] + (value[size : 2 * size] + value[2 * size :])


def below(width, rank, axis):
    shape = (width, 1) if axis == 0 else (1, width)
    return (lax.broadcasted_iota(jnp.int32, shape, axis) < rank).astype(F32)


def pack_kernel(shares, rank_ref, u_ref, v_ref, inverse_ref, *outs):
    width = u_ref.shape[2]
    for tile in range(2):
        out_ref = outs[tile]
        keep = below(width, rank_ref[0, tile], 0)
        out_ref[0] = u_ref[tile, 0]
        out_ref[1] = (v_ref[tile, 0].astype(F32) * keep).astype(BF16)
    rows = outs[2].shape[0]
    start = lax.rem(lax.axis_index("row"), shares) * rows
    outs[2][...] = inverse_ref[pl.ds(pl.multiple_of(start, rows), rows), :]


def join_kernel(*refs):
    for index, ref in enumerate(refs[:-1]):
        refs[-1][index] = ref[...]


def small_kernel(columns, rank_ref, v_ref, w_ref, out_ref):
    width = v_ref.shape[3]
    for c in range(columns):
        rank = rank_ref[0, 0, c]
        value = contract(w_ref[c, 0, 0], v_ref[c, 0, 0], NT)
        out_ref[c] = value * below(width, rank, 0) * below(width, rank, 1)


def eliminate(blocks):
    size = blocks[0].shape[0]
    count = size // GROUP
    unit = (
        lax.broadcasted_iota(jnp.int32, (size, size), 1)
        == lax.broadcasted_iota(jnp.int32, (size, size), 0)
    ).astype(F32)
    shape = (GROUP, 2 * size)
    sub = lax.broadcasted_iota(jnp.int32, shape, 0)
    held = []
    for block in blocks:
        both = jnp.concatenate([block, unit], axis=1)
        held.append([both[g * GROUP : (g + 1) * GROUP] for g in range(count)])

    def row_of(value, index):
        return jnp.broadcast_to(value[index : index + 1, :], shape)

    for g in range(count):
        for rows in held:
            columns = []
            for j in range(GROUP):
                spot = g * GROUP + j
                columns.append(
                    [jnp.broadcast_to(rows[h][:, spot : spot + 1], shape) for h in range(g, count)]
                )
            roots = []
            for j in range(GROUP):
                root = lax.rsqrt(row_of(columns[j][0], j))
                scaled = [value * root for value in columns[j]]
                scaled[0] = jnp.where(sub > j, scaled[0], 0.0)
                columns[j] = scaled
                roots.append(root)
                for k in range(j + 1, GROUP):
                    weight = row_of(scaled[0], k)
                    columns[k] = [a - b * weight for a, b in zip(columns[k], scaled)]
            top = rows[g]
            done = []
            for j in range(GROUP):
                row = row_of(top, j) * roots[j]
                done.append(row)
                top = jnp.where(sub == j, row, top - columns[j][0] * row)
            rows[g] = top
            for h in range(g + 1, count):
                for j in range(GROUP):
                    rows[h] = rows[h] - columns[j][h - g] * done[j]
    return [jnp.concatenate(rows, axis=0)[:, size:] for rows in held]


def block_sizes(width):
    sizes = []
    while width > 0:
        sizes.append(min(64, width))
        width -= sizes[-1]
    return sizes


def inverse_factors(grams):
    width = grams[0].shape[0]
    unit = (
        lax.broadcasted_iota(jnp.int32, (width, width), 0)
        == lax.broadcasted_iota(jnp.int32, (width, width), 1)
    ).astype(F32)
    rests = list(grams)
    sides = [unit for _ in grams]
    found = [[] for _ in grams]
    for size in block_sizes(width):
        smalls = eliminate([rest[:size, :size] for rest in rests])
        for index, small in enumerate(smalls):
            rest, side = rests[index], sides[index]
            right = contract(small, side[:size], NN, HIGH)
            found[index].append(right)
            if rest.shape[0] > size:
                down = contract(rest[size:, :size], small, NT, HIGH)
                across = contract(small, rest[:size, size:], NN, HIGH)
                rests[index] = rest[size:, size:] - contract(down, across, NN, HIGH)
                sides[index] = side[size:] - contract(down, right, NN, HIGH)
    return [jnp.concatenate(rows, axis=0) for rows in found]


def spread_place(value, n_col):
    return value % 2 * (n_col // 2) + value // 2


def gather_place(value, n_col):
    return lax.rem(value, n_col // 2) * 2 + lax.div(value, n_col // 2)


def tile_kernel(n_row, n_col, columns, shares, rank_ref, small_ref, u_ref, v_ref, w_ref, inverse_ref, *refs):
    far, near, refs = refs[:n_row], refs[n_row : n_row + n_col], refs[n_row + n_col :]
    pieces, refs = refs[:shares], refs[shares:]
    new_u_ref, new_v_ref, cu, cv, ru, rv, full, y_ref, sem, share_sem, own_sem = refs
    here = (lax.axis_index("row"), lax.axis_index("col"))
    rows = full.shape[2]
    copies = []
    for flip in range(shares):
        spot = lax.rem(lax.bitwise_xor(here[0], flip), shares)
        for shift in range(1, n_col):
            plane = lax.rem(here[1] - shift + n_col, n_col)
            copies.append(
                pltpu.make_async_copy(
                    pieces[flip].at[shift - 1], full.at[plane, spot], share_sem.at[flip, shift - 1]
                )
            )
    for share in range(shares):
        copies.append(
            pltpu.make_async_copy(
                inverse_ref.at[pl.ds(share * rows, rows)], full.at[here[1], share], own_sem.at[share]
            )
        )
    for flip in range(n_row):
        source = lax.bitwise_xor(here[0], flip)
        chunk_of = lax.bitwise_xor(gather_place(lax.rem(source, n_col), n_col), here[1])
        spot = (lax.div(source, n_col), chunk_of)
        for index, room in enumerate((cu, cv)):
            copies.append(
                pltpu.make_async_copy(
                    far[flip].at[index], room.at[spot], sem.at[index, flip]
                )
            )
    for shift in range(n_col):
        source = lax.rem(here[1] - shift + n_col, n_col)
        for index, room in enumerate((ru, rv)):
            copies.append(
                pltpu.make_async_copy(
                    near[shift].at[index], room.at[source], sem.at[index, n_row + shift]
                )
            )
    for copy in copies:
        copy.start()
    width, height = u_ref.shape[3:]
    chunk = height // n_col
    spans = [slice(a * chunk, (a + 1) * chunk) for a in range(n_col)]
    eye = lax.broadcasted_iota(jnp.int32, (width, width), 0) == lax.broadcasted_iota(
        jnp.int32, (width, width), 1
    )
    across = [below(width, rank_ref[0, 0, c], 1) for c in range(columns)]
    own_parts = [stacked(small_ref[c]) for c in range(columns)]
    for copy in copies:
        copy.wait()
    couplings, far_parts = [], []
    panels = jnp.concatenate(
        [
            jnp.concatenate([cv[c, a] for c in range(columns)] + [rv[a]], axis=0)
            for a in range(n_col)
        ],
        axis=1,
    )
    solved = []
    for a in range(n_col):
        end = (a + 1) * chunk
        piece = full[a].reshape(chunk, height)[:, :end]
        solved.append(contract(panels[:, :end], piece, NT).astype(BF16))
    for c in range(columns):
        coupling = sum(
            contract(value[columns * width :], value[c * width : (c + 1) * width], NT)
            for value in solved
        )
        right = sum(contract(w_ref[c, 0, 0, :, spans[a]], cu[c, a], NT) for a in range(n_col))
        couplings.append(coupling)
        right = right * below(width, rank_ref[0, 0, c], 0)
        far_parts.append(stacked(-contract(right, coupling, NT, HIGH)))
    grams = [jnp.where(eye, 1.0 - across[c], 0.0) for c in range(columns)]
    for a in range(n_col):
        for c in range(columns):
            y = folded(
                contract(own_parts[c], u_ref[c, 0, 0, :, spans[a]], NN)
                + contract(far_parts[c], ru[a], NN)
            )
            y_ref[c, a] = y
            grams[c] = grams[c] + contract(y, y, NT, HIGH)
    inverses = inverse_factors(grams)
    own = [jnp.zeros((3 * width, width), F32) for _ in range(columns)]
    far = [jnp.zeros((3 * width, width), F32) for _ in range(columns)]
    for a in range(n_col):
        for c in range(columns):
            y = stacked(y_ref[c, a])
            own[c] = own[c] + contract(y, u_ref[c, 0, 0, :, spans[a]], NT)
            far[c] = far[c] + contract(y, ru[a], NT)
    factor = math.sqrt(height)
    for c in range(columns):
        scaled = inverses[c] * factor
        for a in range(n_col):
            new_u_ref[c, 0, 0, :, spans[a]] = contract(scaled, y_ref[c, a], NN, HIGH)
        scaled = inverses[c] * (1.0 / factor)
        left = contract(scaled, folded(own[c]) * across[c], NN, HIGH)
        right = contract(scaled, -folded(far[c]), NN, HIGH)
        left, right = stacked(left), stacked(contract(right, couplings[c], NN, HIGH))
        for a in range(n_col):
            new_v_ref[c, 0, 0, :, spans[a]] = folded(
                contract(left, v_ref[c, 0, 0, :, spans[a]], NN) + contract(right, cu[c, a], NN)
            )


def share_count(n_row, chunk):
    return max(1, min(n_row, chunk // SHARE_ROWS))


def whole(panel_u, panel_v, panel_rank, diag_inverse, tile_u, tile_v, tile_rank, sketch):
    n_row, n_col = lax.axis_size("row"), lax.axis_size("col")
    panel_u, panel_v, tile_u, tile_v, sketch = (
        jnp.swapaxes(value, -1, -2) for value in (panel_u, panel_v, tile_u, tile_v, sketch)
    )
    panel_rank, tile_rank = jnp.swapaxes(panel_rank, 0, 1), jnp.moveaxis(tile_rank, 0, -1)
    width, chunk = panel_u.shape[2:]
    columns = tile_u.shape[0]
    pair = jax.ShapeDtypeStruct((2, width, chunk), BF16)

    def across(value):
        pairs = []
        for row in range(n_row):
            for col in range(n_col):
                spot = spread_place(row % n_col ^ col, n_col)
                pairs.append((row * n_col + col, (row // n_col * n_col + spot) * n_col + row % n_col))
        return lax.ppermute(value, ("row", "col"), pairs)

    def flip(value, mask):
        return lax.ppermute(value, "row", [(i, i ^ mask) for i in range(n_row)])

    def plane(value, count):
        same = {0: value}
        for mask in range(2, count, 2):
            same[mask] = flip(value, mask)
        full = dict(same)
        for mask in range(0, count, 2):
            full[mask + 1] = flip(same[mask], 1)
        return [full[mask] for mask in range(count)]

    def along(value):
        found = [value]
        for shift in range(1, n_col):
            pairs = [(i, (i + shift) % n_col) for i in range(n_col)]
            found.append(lax.ppermute(value, "col", pairs))
        return found

    shares = share_count(n_row, chunk)
    part = jax.ShapeDtypeStruct((chunk // shares, diag_inverse.shape[1]), BF16)
    far, near, share = pl.pallas_call(
        functools.partial(pack_kernel, shares),
        out_shape=(pair, pair, part),
        in_specs=[SMEM] + [VMEM] * 3,
        out_specs=(VMEM,) * 3,
        name="pack",
    )(panel_rank, panel_u, panel_v, diag_inverse)
    far, shared = across(far), along(share)[1:]
    near, far = along(near), plane(far, n_row)
    joined = pl.pallas_call(
        join_kernel,
        out_shape=jax.ShapeDtypeStruct((n_col - 1,) + share.shape, BF16),
        in_specs=[VMEM] * (n_col - 1),
        out_specs=VMEM,
        name="join",
    )(*shared)
    pieces = plane(joined, shares)
    small = pl.pallas_call(
        functools.partial(small_kernel, columns),
        out_shape=jax.ShapeDtypeStruct((columns, width, width), F32),
        in_specs=[SMEM, VMEM, VMEM],
        out_specs=VMEM,
        name="small",
    )(tile_rank, tile_v, sketch)
    room = pltpu.VMEM((columns, n_col, width, chunk), BF16)
    near_room = pltpu.VMEM((n_col, width, chunk), BF16)
    result = jax.ShapeDtypeStruct(tile_u.shape, F32)
    new_u, new_v = pl.pallas_call(
        functools.partial(tile_kernel, n_row, n_col, columns, shares),
        out_shape=(result, result),
        in_specs=[SMEM] + [VMEM] * 4 + [HBM] * (1 + n_row + n_col + shares),
        out_specs=(VMEM, VMEM),
        scratch_shapes=[
            room,
            room,
            near_room,
            near_room,
            pltpu.VMEM((n_col, shares) + share.shape, BF16),
            pltpu.VMEM((columns, n_col, width, chunk), F32),
            pltpu.SemaphoreType.DMA((2, n_row + n_col)),
            pltpu.SemaphoreType.DMA((shares, n_col - 1)),
            pltpu.SemaphoreType.DMA((shares,)),
        ],
        compiler_params=pltpu.CompilerParams(vmem_limit_bytes=60 * 1024 * 1024),
        name="tiles",
    )(tile_rank, small, tile_u, tile_v, sketch, diag_inverse, *far, *near, *pieces)
    return jnp.swapaxes(new_u, -1, -2), jnp.swapaxes(new_v, -1, -2)


def solution(mesh):
    n_row, n_col = mesh.shape["row"], mesh.shape["col"]
    assert n_row % n_col == 0
    wide = P(None, "row", "col", None)
    tile = P(None, "row", "col", None, None)
    return jax.shard_map(
        whole,
        mesh=mesh,
        in_specs=(wide, wide, P(None, "row"), P("col", None), tile, tile, P(None, "row", "col"), tile),
        out_specs=(tile, tile),
        check_vma=False,
    )
```

profile of v0, /device:TPU:0, one launch (start us, length us, event | category | flops | bytes accessed | tf_op | source)
XLA Modules:
  0.0 79.4 jit_solution(13217610180512574888)
XLA Ops:
  0.6 2.0 %pack.1 = (bf16[2,160,256]{2,1,0:T(8,128)(2,1)}, bf16[2,160,256]{2,1,0:T(8,128)(2,1)}, bf16[32,1024]{1,0:T(8,128)(2,1)}) custom-call(s32[1,2]{1,0:T(1,128)} %bitcast.18, bf16[2,1,160,256]{3,2,1,0:T(8,128)(2,1)} %bitcast.14, bf16[2,1,160,256]{3,2,1,0:T(8,128)(2,1)} %bitcast.15, bf16[256,1024]{1,0:T(8,128)(2,1)} %inverse_ref.3), custom_call_target="tpu_custom_call" | custom-call | tf_op jit(solution)/shard_map/pack/pallas_call | solution.py:309
  2.6 5.1 %collective-permute-start.13 = (bf16[32,1024]{1,0:T(8,128)(2,1)}, bf16[32,1024]{1,0:T(8,128)(2,1)S(1)}, u32[]{:S(2)}, u32[]{:S(2)}) collective-permute-start(bf16[32,1024]{1,0:T(8,128)(2,1)} %get-tuple-element.9), channel_id=1, source_target_pairs={{0,3},{1,0},{2,1},{3,2},{4,7},{5,4},{6,5},{7,6},{8,11},{9,8},{10,9... | collective-permute-start | bytes 196616 | tf_op jit(solution)/shard_map/ppermute | solution.py:304
  7.7 1.6 %collective-permute-start = (bf16[2,160,256]{2,1,0:T(8,128)(2,1)}, bf16[2,160,256]{2,1,0:T(8,128)(2,1)S(1)}, u32[]{:S(2)}, u32[]{:S(2)}) collective-permute-start(bf16[2,160,256]{2,1,0:T(8,128)(2,1)} %get-tuple-element.7), channel_id=1, source_target_pairs={{0,0},{1,8},{2,4},{3,12},{4,9},{5,1},{6,13},{7,5},{8,6},{9,14},{10... | collective-permute-start | bytes 491528 | tf_op jit(solution)/shard_map/ppermute | solution.py:286
  9.3 4.3 %collective-permute-start.10 = (bf16[2,160,256]{2,1,0:T(8,128)(2,1)}, bf16[2,160,256]{2,1,0:T(8,128)(2,1)S(1)}, u32[]{:S(2)}, u32[]{:S(2)}) collective-permute-start(bf16[2,160,256]{2,1,0:T(8,128)(2,1)} %get-tuple-element.8.refs_8_), channel_id=1, source_target_pairs={{0,3},{1,0},{2,1},{3,2},{4,7},{5,4},{6,5},{7,6},{8,11},{9,8},{10,9... | collective-permute-start | bytes 491528 | tf_op jit(solution)/shard_map/ppermute | solution.py:304
  13.6 0.5 collective-permute-start.9
  14.1 2.4 %collective-permute-start.12 = (bf16[32,1024]{1,0:T(8,128)(2,1)}, bf16[32,1024]{1,0:T(8,128)(2,1)S(1)}, u32[]{:S(2)}, u32[]{:S(2)}) collective-permute-start(bf16[32,1024]{1,0:T(8,128)(2,1)} %get-tuple-element.9), channel_id=1, source_target_pairs={{0,2},{1,3},{2,0},{3,1},{4,6},{5,7},{6,4},{7,5},{8,10},{9,11},{10,... | collective-permute-start | bytes 196616 | tf_op jit(solution)/shard_map/ppermute | solution.py:304
  16.5 0.0 collective-permute-done.13.refs_2_
  16.5 0.0 collective-permute-start.11
  16.5 15.9 %collective-permute-done.12.refs_1_ = bf16[32,1024]{1,0:T(8,128)(2,1)S(1)} collective-permute-done((bf16[32,1024]{1,0:T(8,128)(2,1)}, bf16[32,1024]{1,0:T(8,128)(2,1)S(1)}, u32[]{:S(2)}, u32[]{:S(2)}) %collective-permute-start.12) | collective-permute-done | bytes 65568 | tf_op jit(solution)/shard_map/ppermute | solution.py:304
  32.4 0.0 collective-permute-done.11.refs_0_
  32.4 0.0 copy-done.18
  32.4 0.6 copy-done.19
  33.0 0.6 copy-done.20
  33.7 1.6 %join.1.refs_12_ = bf16[3,32,1024]{2,1,0:T(8,128)(2,1)} custom-call(bf16[32,1024]{1,0:T(8,128)(2,1)} %copy-done.20, bf16[32,1024]{1,0:T(8,128)(2,1)} %copy-done.19, bf16[32,1024]{1,0:T(8,128)(2,1)} %copy-done.18), custom_call_target="tpu_custom_call" | custom-call | tf_op jit(solution)/shard_map/join/pallas_call | solution.py:318
  35.3 0.0 collective-permute-start.19
  35.3 1.6 %collective-permute-start.17 = (bf16[3,32,1024]{2,1,0:T(8,128)(2,1)}, bf16[3,32,1024]{2,1,0:T(8,128)(2,1)S(1)}, u32[]{:S(2)}, u32[]{:S(2)}) collective-permute-start(bf16[3,32,1024]{2,1,0:T(8,128)(2,1)} %join.1.refs_12_), channel_id=1, source_target_pairs={{0,16},{4,20},{8,24},{12,28},{16,0},{20,4},{24,8},{28,12},{1,17},{... | collective-permute-start | bytes 589832 | tf_op jit(solution)/shard_map/ppermute | solution.py:289
  36.8 0.0 collective-permute-done.refs_0_
  36.8 0.6 collective-permute-start.8
  37.4 0.0 collective-permute-done.10.refs_11_
  37.4 1.5 %collective-permute-start.15 = (bf16[3,32,1024]{2,1,0:T(8,128)(2,1)}, bf16[3,32,1024]{2,1,0:T(8,128)(2,1)S(1)}, u32[]{:S(2)}, u32[]{:S(2)}) collective-permute-start(bf16[3,32,1024]{2,1,0:T(8,128)(2,1)} %join.1.refs_12_), channel_id=1, source_target_pairs={{0,8},{4,12},{8,0},{12,4},{16,24},{20,28},{24,16},{28,20},{1,9},{5... | collective-permute-start | bytes 589832 | tf_op jit(solution)/shard_map/ppermute | solution.py:289
  38.9 0.0 collective-permute-done.9.refs_10_
  38.9 0.0 collective-permute-start.14
  38.9 5.3 %collective-permute-done.8.refs_9_ = bf16[2,160,256]{2,1,0:T(8,128)(2,1)S(1)} collective-permute-done((bf16[2,160,256]{2,1,0:T(8,128)(2,1)}, bf16[2,160,256]{2,1,0:T(8,128)(2,1)S(1)}, u32[]{:S(2)}, u32[]{:S(2)}) %collective-permute-start.8) | collective-permute-done | bytes 163872 | tf_op jit(solution)/shard_map/ppermute | solution.py:304
  44.2 2.9 %collective-permute-start.6 = (bf16[2,160,256]{2,1,0:T(8,128)(2,1)S(1)}, bf16[2,160,256]{2,1,0:T(8,128)(2,1)S(1)}, u32[]{:S(2)}, u32[]{:S(2)}) collective-permute-start(bf16[2,160,256]{2,1,0:T(8,128)(2,1)S(1)} %collective-permute-done.refs_0_), channel_id=1, source_target_pairs={{0,24},{4,28},{8,16},{12,20},{16,8},{20,12},{24,0},{28,4},{1,25},{... | collective-permute-start | bytes 491528 | tf_op jit(solution)/shard_map/ppermute | solution.py:289
  47.1 0.0 collective-permute-done.19.refs_18_
  47.1 0.5 collective-permute-start.4
  47.6 0.0 collective-permute-done.17.refs_16_
  47.6 0.0 collective-permute-start.20
  47.6 0.0 collective-permute-done.15.refs_14_
  47.6 0.0 copy-start.2
  47.6 0.2 collective-permute-start.2
  47.8 0.0 collective-permute-done.14.refs_13_
  47.8 0.3 collective-permute-start.1
  48.2 3.2 %collective-permute-done.6.refs_6_ = bf16[2,160,256]{2,1,0:T(8,128)(2,1)S(1)} collective-permute-done((bf16[2,160,256]{2,1,0:T(8,128)(2,1)S(1)}, bf16[2,160,256]{2,1,0:T(8,128)(2,1)S(1)}, u32[]{:S(2)}, u32[]{:S(2)}) %collective-permute-start.6) | collective-permute-done | bytes 163872 | tf_op jit(solution)/shard_map/ppermute | solution.py:289
  51.4 0.0 collective-permute-start.18
  51.4 1.8 %collective-permute-done.4.refs_4_ = bf16[2,160,256]{2,1,0:T(8,128)(2,1)S(1)} collective-permute-done((bf16[2,160,256]{2,1,0:T(8,128)(2,1)S(1)}, bf16[2,160,256]{2,1,0:T(8,128)(2,1)S(1)}, u32[]{:S(2)}, u32[]{:S(2)}) %collective-permute-start.4) | collective-permute-done | bytes 163872 | tf_op jit(solution)/shard_map/ppermute | solution.py:289
  53.2 0.0 collective-permute-start.16
  53.2 1.0 %collective-permute-done.2.refs_2_ = bf16[2,160,256]{2,1,0:T(8,128)(2,1)S(1)} collective-permute-done((bf16[2,160,256]{2,1,0:T(8,128)(2,1)S(1)}, bf16[2,160,256]{2,1,0:T(8,128)(2,1)S(1)}, u32[]{:S(2)}, u32[]{:S(2)}) %collective-permute-start.2) | collective-permute-done | bytes 163872 | tf_op jit(solution)/shard_map/ppermute | solution.py:289
  54.2 0.0 collective-permute-start.7
  54.2 0.0 collective-permute-done.1.refs_1_
  54.2 0.0 copy-start.14
  54.2 0.5 collective-permute-start.5
  54.7 0.0 collective-permute-done.20.refs_19_
  54.7 0.1 collective-permute-start.3
  54.8 2.4 %small.1.small_ref = f32[2,160,160]{2,1,0:T(8,128)} custom-call(s32[1,1,2]{2,1,0:T(1,128)} %bitcast.16, bf16[2,1,1,160,1024]{4,3,2,1,0:T(8,128)(2,1)} %bitcast.9, bf16[2,1,1,160,1024]{4,3,2,1,0:T(8,128)(2,1)} %bitcast.11), custom_call_target="tpu_custom_call" | custom-call | tf_op jit(solution)/shard_map/small/pallas_call | solution.py:326
  57.2 0.0 collective-permute-done.18.refs_17_
  57.2 0.0 collective-permute-done.16.refs_15_
  57.2 0.0 copy-start.6
  57.2 0.0 collective-permute-done.7.refs_7_
  57.2 0.0 copy-start.15
  57.2 0.0 collective-permute-done.5.refs_5_
  57.2 0.0 copy-start.16
  57.2 0.0 collective-permute-done.3.refs_3_
  57.2 0.0 copy-start.17
  57.3 0.0 copy-done.7
  57.3 0.0 copy-done.8
  57.3 0.0 copy-done.9
  57.3 0.0 copy-done.10
  57.4 0.5 copy-done.5
  57.9 0.1 copy-done.6
  57.9 0.1 copy-done.15
  58.0 0.1 copy-done.16
  58.1 0.0 copy-done.17
  58.1 21.3 %tiles.1 = (f32[2,1,1,160,1024]{4,3,2,1,0:T(8,128)}, f32[2,1,1,160,1024]{4,3,2,1,0:T(8,128)}) custom-call(s32[1,1,2]{2,1,0:T(1,128)} %bitcast.17, f32[2,160,160]{2,1,0:T(8,128)} %small.1.small_ref, bf16[2,1,1,160,1024]{4,3,2,1,0:T(8,128)(2,1)} %bitcast.13, bf16[2,1,1,160,1024]{4,3,2,1,0:T(8,128)(2,1)} %bitcast.10, bf16[2,1,1,160,1024]{4,3,2,1,0:T(8,128)(2,1)} %bitcast.12, ...), custom_call_target="tpu_custom_call" | custom-call | tf_op jit(solution)/shard_map/tiles/pallas_call | solution.py:336
  (24 shorter events, 0.0 us)
Async XLA Ops:
  2.6 13.9 %collective-permute-start.13 = (bf16[32,1024]{1,0:T(8,128)(2,1)}, bf16[32,1024]{1,0:T(8,128)(2,1)S(1)}, u32[]{:S(2)}, u32[]{:S(2)}) collective-permute-start(bf16[32,1024]{1,0:T(8,128)(2,1)} %get-tuple-element.9), channel_id=1, source_target_pairs={{0,3},{1,0},{2,1},{3,2},{4,7},{5,4},{6,5},{7,6},{8,11},{9,8},{10,9... | collective-permute-start | bytes 196616 | tf_op jit(solution)/shard_map/ppermute | solution.py:304
  7.7 29.1 %collective-permute-start = (bf16[2,160,256]{2,1,0:T(8,128)(2,1)}, bf16[2,160,256]{2,1,0:T(8,128)(2,1)S(1)}, u32[]{:S(2)}, u32[]{:S(2)}) collective-permute-start(bf16[2,160,256]{2,1,0:T(8,128)(2,1)} %get-tuple-element.7), channel_id=1, source_target_pairs={{0,0},{1,8},{2,4},{3,12},{4,9},{5,1},{6,13},{7,5},{8,6},{9,14},{10... | collective-permute-start | bytes 491528 | tf_op jit(solution)/shard_map/ppermute | solution.py:286
  9.3 28.1 %collective-permute-start.10 = (bf16[2,160,256]{2,1,0:T(8,128)(2,1)}, bf16[2,160,256]{2,1,0:T(8,128)(2,1)S(1)}, u32[]{:S(2)}, u32[]{:S(2)}) collective-permute-start(bf16[2,160,256]{2,1,0:T(8,128)(2,1)} %get-tuple-element.8.refs_8_), channel_id=1, source_target_pairs={{0,3},{1,0},{2,1},{3,2},{4,7},{5,4},{6,5},{7,6},{8,11},{9,8},{10,9... | collective-permute-start | bytes 491528 | tf_op jit(solution)/shard_map/ppermute | solution.py:304
  13.6 25.3 %collective-permute-start.9 = (bf16[2,160,256]{2,1,0:T(8,128)(2,1)}, bf16[2,160,256]{2,1,0:T(8,128)(2,1)S(1)}, u32[]{:S(2)}, u32[]{:S(2)}) collective-permute-start(bf16[2,160,256]{2,1,0:T(8,128)(2,1)} %get-tuple-element.8.refs_8_), channel_id=1, source_target_pairs={{0,2},{1,3},{2,0},{3,1},{4,6},{5,7},{6,4},{7,5},{8,10},{9,11},{10,... | collective-permute-start | bytes 491528 | tf_op jit(solution)/shard_map/ppermute | solution.py:304
  14.1 18.4 %collective-permute-start.12 = (bf16[32,1024]{1,0:T(8,128)(2,1)}, bf16[32,1024]{1,0:T(8,128)(2,1)S(1)}, u32[]{:S(2)}, u32[]{:S(2)}) collective-permute-start(bf16[32,1024]{1,0:T(8,128)(2,1)} %get-tuple-element.9), channel_id=1, source_target_pairs={{0,2},{1,3},{2,0},{3,1},{4,6},{5,7},{6,4},{7,5},{8,10},{9,11},{10,... | collective-permute-start | bytes 196616 | tf_op jit(solution)/shard_map/ppermute | solution.py:304
  16.5 15.9 %copy-start.18 = (bf16[32,1024]{1,0:T(8,128)(2,1)}, bf16[32,1024]{1,0:T(8,128)(2,1)S(1)}, u32[]{:S(2)}) copy-start(bf16[32,1024]{1,0:T(8,128)(2,1)S(1)} %collective-permute-done.13.refs_2_) | copy-start | bytes 196612
  16.5 15.9 %collective-permute-start.11 = (bf16[32,1024]{1,0:T(8,128)(2,1)}, bf16[32,1024]{1,0:T(8,128)(2,1)S(1)}, u32[]{:S(2)}, u32[]{:S(2)}) collective-permute-start(bf16[32,1024]{1,0:T(8,128)(2,1)} %get-tuple-element.9), channel_id=1, source_target_pairs={{0,1},{1,2},{2,3},{3,0},{4,5},{5,6},{6,7},{7,4},{8,9},{9,10},{10,1... | collective-permute-start | bytes 196616 | tf_op jit(solution)/shard_map/ppermute | solution.py:304
  32.4 0.6 copy-start.19
  33.0 0.6 copy-start.20
  35.3 11.8 %collective-permute-start.19 = (bf16[3,32,1024]{2,1,0:T(8,128)(2,1)}, bf16[3,32,1024]{2,1,0:T(8,128)(2,1)S(1)}, u32[]{:S(2)}, u32[]{:S(2)}) collective-permute-start(bf16[3,32,1024]{2,1,0:T(8,128)(2,1)} %join.1.refs_12_), channel_id=1, source_target_pairs={{0,24},{4,28},{8,16},{12,20},{16,8},{20,12},{24,0},{28,4},{1,25},{... | collective-permute-start | bytes 589832 | tf_op jit(solution)/shard_map/ppermute | solution.py:289
  35.3 12.3 %collective-permute-start.17 = (bf16[3,32,1024]{2,1,0:T(8,128)(2,1)}, bf16[3,32,1024]{2,1,0:T(8,128)(2,1)S(1)}, u32[]{:S(2)}, u32[]{:S(2)}) collective-permute-start(bf16[3,32,1024]{2,1,0:T(8,128)(2,1)} %join.1.refs_12_), channel_id=1, source_target_pairs={{0,16},{4,20},{8,24},{12,28},{16,0},{20,4},{24,8},{28,12},{1,17},{... | collective-permute-start | bytes 589832 | tf_op jit(solution)/shard_map/ppermute | solution.py:289
  36.8 20.4 %copy-start.7 = (bf16[2,160,256]{2,1,0:T(8,128)(2,1)}, bf16[2,160,256]{2,1,0:T(8,128)(2,1)S(1)}, u32[]{:S(2)}) copy-start(bf16[2,160,256]{2,1,0:T(8,128)(2,1)S(1)} %collective-permute-done.refs_0_) | copy-start | bytes 491524
  36.8 7.3 %collective-permute-start.8 = (bf16[2,160,256]{2,1,0:T(8,128)(2,1)}, bf16[2,160,256]{2,1,0:T(8,128)(2,1)S(1)}, u32[]{:S(2)}, u32[]{:S(2)}) collective-permute-start(bf16[2,160,256]{2,1,0:T(8,128)(2,1)} %get-tuple-element.8.refs_8_), channel_id=1, source_target_pairs={{0,1},{1,2},{2,3},{3,0},{4,5},{5,6},{6,7},{7,4},{8,9},{9,10},{10,1... | collective-permute-start | bytes 491528 | tf_op jit(solution)/shard_map/ppermute | solution.py:304
  37.4 19.9 %copy-start.8 = (bf16[2,160,256]{2,1,0:T(8,128)(2,1)}, bf16[2,160,256]{2,1,0:T(8,128)(2,1)S(1)}, u32[]{:S(2)}) copy-start(bf16[2,160,256]{2,1,0:T(8,128)(2,1)S(1)} %collective-permute-done.10.refs_11_) | copy-start | bytes 491524
  37.4 10.2 %collective-permute-start.15 = (bf16[3,32,1024]{2,1,0:T(8,128)(2,1)}, bf16[3,32,1024]{2,1,0:T(8,128)(2,1)S(1)}, u32[]{:S(2)}, u32[]{:S(2)}) collective-permute-start(bf16[3,32,1024]{2,1,0:T(8,128)(2,1)} %join.1.refs_12_), channel_id=1, source_target_pairs={{0,8},{4,12},{8,0},{12,4},{16,24},{20,28},{24,16},{28,20},{1,9},{5... | collective-permute-start | bytes 589832 | tf_op jit(solution)/shard_map/ppermute | solution.py:289
  38.9 18.4 %copy-start.9 = (bf16[2,160,256]{2,1,0:T(8,128)(2,1)}, bf16[2,160,256]{2,1,0:T(8,128)(2,1)S(1)}, u32[]{:S(2)}) copy-start(bf16[2,160,256]{2,1,0:T(8,128)(2,1)S(1)} %collective-permute-done.9.refs_10_) | copy-start | bytes 491524
  38.9 9.0 %collective-permute-start.14 = (bf16[3,32,1024]{2,1,0:T(8,128)(2,1)}, bf16[3,32,1024]{2,1,0:T(8,128)(2,1)S(1)}, u32[]{:S(2)}, u32[]{:S(2)}) collective-permute-start(bf16[3,32,1024]{2,1,0:T(8,128)(2,1)} %join.1.refs_12_), channel_id=1, source_target_pairs={{0,4},{4,0},{8,12},{12,8},{16,20},{20,16},{24,28},{28,24},{1,5},{5... | collective-permute-start | bytes 589832 | tf_op jit(solution)/shard_map/ppermute | solution.py:289
  44.2 13.1 %copy-start.10 = (bf16[2,160,256]{2,1,0:T(8,128)(2,1)}, bf16[2,160,256]{2,1,0:T(8,128)(2,1)S(1)}, u32[]{:S(2)}) copy-start(bf16[2,160,256]{2,1,0:T(8,128)(2,1)S(1)} %collective-permute-done.8.refs_9_) | copy-start | bytes 491524
  44.2 7.2 %collective-permute-start.6 = (bf16[2,160,256]{2,1,0:T(8,128)(2,1)S(1)}, bf16[2,160,256]{2,1,0:T(8,128)(2,1)S(1)}, u32[]{:S(2)}, u32[]{:S(2)}) collective-permute-start(bf16[2,160,256]{2,1,0:T(8,128)(2,1)S(1)} %collective-permute-done.refs_0_), channel_id=1, source_target_pairs={{0,24},{4,28},{8,16},{12,20},{16,8},{20,12},{24,0},{28,4},{1,25},{... | collective-permute-start | bytes 491528 | tf_op jit(solution)/shard_map/ppermute | solution.py:289
  47.1 10.2 %copy-start = (bf16[3,32,1024]{2,1,0:T(8,128)(2,1)}, bf16[3,32,1024]{2,1,0:T(8,128)(2,1)S(1)}, u32[]{:S(2)}) copy-start(bf16[3,32,1024]{2,1,0:T(8,128)(2,1)S(1)} %collective-permute-done.19.refs_18_) | copy-start | bytes 589828
  47.1 6.1 %collective-permute-start.4 = (bf16[2,160,256]{2,1,0:T(8,128)(2,1)S(1)}, bf16[2,160,256]{2,1,0:T(8,128)(2,1)S(1)}, u32[]{:S(2)}, u32[]{:S(2)}) collective-permute-start(bf16[2,160,256]{2,1,0:T(8,128)(2,1)S(1)} %collective-permute-done.refs_0_), channel_id=1, source_target_pairs={{0,16},{4,20},{8,24},{12,28},{16,0},{20,4},{24,8},{28,12},{1,17},{... | collective-permute-start | bytes 491528 | tf_op jit(solution)/shard_map/ppermute | solution.py:289
  47.6 9.7 %copy-start.1 = (bf16[3,32,1024]{2,1,0:T(8,128)(2,1)}, bf16[3,32,1024]{2,1,0:T(8,128)(2,1)S(1)}, u32[]{:S(2)}) copy-start(bf16[3,32,1024]{2,1,0:T(8,128)(2,1)S(1)} %collective-permute-done.17.refs_16_) | copy-start | bytes 589828
  47.6 7.1 %collective-permute-start.20 = (bf16[3,32,1024]{2,1,0:T(8,128)(2,1)S(1)}, bf16[3,32,1024]{2,1,0:T(8,128)(2,1)S(1)}, u32[]{:S(2)}, u32[]{:S(2)}) collective-permute-start(bf16[3,32,1024]{2,1,0:T(8,128)(2,1)S(1)} %collective-permute-done.19.refs_18_), channel_id=1, source_target_pairs={{0,4},{4,0},{8,12},{12,8},{16,20},{20,16},{24,28},{28,24},{1,5},{5... | collective-permute-start | bytes 589832 | tf_op jit(solution)/shard_map/ppermute | solution.py:289
  47.6 9.7 %copy-start.2 = (bf16[3,32,1024]{2,1,0:T(8,128)(2,1)}, bf16[3,32,1024]{2,1,0:T(8,128)(2,1)S(1)}, u32[]{:S(2)}) copy-start(bf16[3,32,1024]{2,1,0:T(8,128)(2,1)S(1)} %collective-permute-done.15.refs_14_) | copy-start | bytes 589828
  47.6 6.6 %collective-permute-start.2 = (bf16[2,160,256]{2,1,0:T(8,128)(2,1)S(1)}, bf16[2,160,256]{2,1,0:T(8,128)(2,1)S(1)}, u32[]{:S(2)}, u32[]{:S(2)}) collective-permute-start(bf16[2,160,256]{2,1,0:T(8,128)(2,1)S(1)} %collective-permute-done.refs_0_), channel_id=1, source_target_pairs={{0,8},{4,12},{8,0},{12,4},{16,24},{20,28},{24,16},{28,20},{1,9},{5... | collective-permute-start | bytes 491528 | tf_op jit(solution)/shard_map/ppermute | solution.py:289
  47.8 9.5 %copy-start.3 = (bf16[3,32,1024]{2,1,0:T(8,128)(2,1)}, bf16[3,32,1024]{2,1,0:T(8,128)(2,1)S(1)}, u32[]{:S(2)}) copy-start(bf16[3,32,1024]{2,1,0:T(8,128)(2,1)S(1)} %collective-permute-done.14.refs_13_) | copy-start | bytes 589828
  47.8 6.4 %collective-permute-start.1 = (bf16[2,160,256]{2,1,0:T(8,128)(2,1)S(1)}, bf16[2,160,256]{2,1,0:T(8,128)(2,1)S(1)}, u32[]{:S(2)}, u32[]{:S(2)}) collective-permute-start(bf16[2,160,256]{2,1,0:T(8,128)(2,1)S(1)} %collective-permute-done.refs_0_), channel_id=1, source_target_pairs={{0,4},{4,0},{8,12},{12,8},{16,20},{20,16},{24,28},{28,24},{1,5},{5... | collective-permute-start | bytes 491528 | tf_op jit(solution)/shard_map/ppermute | solution.py:289
  51.4 6.0 %copy-start.11 = (bf16[2,160,256]{2,1,0:T(8,128)(2,1)}, bf16[2,160,256]{2,1,0:T(8,128)(2,1)S(1)}, u32[]{:S(2)}) copy-start(bf16[2,160,256]{2,1,0:T(8,128)(2,1)S(1)} %collective-permute-done.6.refs_6_) | copy-start | bytes 491524
  51.4 5.8 %collective-permute-start.18 = (bf16[3,32,1024]{2,1,0:T(8,128)(2,1)S(1)}, bf16[3,32,1024]{2,1,0:T(8,128)(2,1)S(1)}, u32[]{:S(2)}, u32[]{:S(2)}) collective-permute-start(bf16[3,32,1024]{2,1,0:T(8,128)(2,1)S(1)} %collective-permute-done.17.refs_16_), channel_id=1, source_target_pairs={{0,4},{4,0},{8,12},{12,8},{16,20},{20,16},{24,28},{28,24},{1,5},{5... | collective-permute-start | bytes 589832 | tf_op jit(solution)/shard_map/ppermute | solution.py:289
  53.2 4.1 %copy-start.12 = (bf16[2,160,256]{2,1,0:T(8,128)(2,1)}, bf16[2,160,256]{2,1,0:T(8,128)(2,1)S(1)}, u32[]{:S(2)}) copy-start(bf16[2,160,256]{2,1,0:T(8,128)(2,1)S(1)} %collective-permute-done.4.refs_4_) | copy-start | bytes 491524
  53.2 4.0 %collective-permute-start.16 = (bf16[3,32,1024]{2,1,0:T(8,128)(2,1)S(1)}, bf16[3,32,1024]{2,1,0:T(8,128)(2,1)S(1)}, u32[]{:S(2)}, u32[]{:S(2)}) collective-permute-start(bf16[3,32,1024]{2,1,0:T(8,128)(2,1)S(1)} %collective-permute-done.15.refs_14_), channel_id=1, source_target_pairs={{0,4},{4,0},{8,12},{12,8},{16,20},{20,16},{24,28},{28,24},{1,5},{5... | collective-permute-start | bytes 589832 | tf_op jit(solution)/shard_map/ppermute | solution.py:289
  54.2 3.2 %copy-start.13 = (bf16[2,160,256]{2,1,0:T(8,128)(2,1)}, bf16[2,160,256]{2,1,0:T(8,128)(2,1)S(1)}, u32[]{:S(2)}) copy-start(bf16[2,160,256]{2,1,0:T(8,128)(2,1)S(1)} %collective-permute-done.2.refs_2_) | copy-start | bytes 491524
  54.2 3.0 %collective-permute-start.7 = (bf16[2,160,256]{2,1,0:T(8,128)(2,1)S(1)}, bf16[2,160,256]{2,1,0:T(8,128)(2,1)S(1)}, u32[]{:S(2)}, u32[]{:S(2)}) collective-permute-start(bf16[2,160,256]{2,1,0:T(8,128)(2,1)S(1)} %collective-permute-done.6.refs_6_), channel_id=1, source_target_pairs={{0,4},{4,0},{8,12},{12,8},{16,20},{20,16},{24,28},{28,24},{1,5},{5... | collective-permute-start | bytes 491528 | tf_op jit(solution)/shard_map/ppermute | solution.py:289
  54.2 3.2 %copy-start.14 = (bf16[2,160,256]{2,1,0:T(8,128)(2,1)}, bf16[2,160,256]{2,1,0:T(8,128)(2,1)S(1)}, u32[]{:S(2)}) copy-start(bf16[2,160,256]{2,1,0:T(8,128)(2,1)S(1)} %collective-permute-done.1.refs_1_) | copy-start | bytes 491524
  54.2 3.0 %collective-permute-start.5 = (bf16[2,160,256]{2,1,0:T(8,128)(2,1)S(1)}, bf16[2,160,256]{2,1,0:T(8,128)(2,1)S(1)}, u32[]{:S(2)}, u32[]{:S(2)}) collective-permute-start(bf16[2,160,256]{2,1,0:T(8,128)(2,1)S(1)} %collective-permute-done.4.refs_4_), channel_id=1, source_target_pairs={{0,4},{4,0},{8,12},{12,8},{16,20},{20,16},{24,28},{28,24},{1,5},{5... | collective-permute-start | bytes 491528 | tf_op jit(solution)/shard_map/ppermute | solution.py:289
  54.7 2.7 %copy-start.4 = (bf16[3,32,1024]{2,1,0:T(8,128)(2,1)}, bf16[3,32,1024]{2,1,0:T(8,128)(2,1)S(1)}, u32[]{:S(2)}) copy-start(bf16[3,32,1024]{2,1,0:T(8,128)(2,1)S(1)} %collective-permute-done.20.refs_19_) | copy-start | bytes 589828
  54.7 2.5 %collective-permute-start.3 = (bf16[2,160,256]{2,1,0:T(8,128)(2,1)S(1)}, bf16[2,160,256]{2,1,0:T(8,128)(2,1)S(1)}, u32[]{:S(2)}, u32[]{:S(2)}) collective-permute-start(bf16[2,160,256]{2,1,0:T(8,128)(2,1)S(1)} %collective-permute-done.2.refs_2_), channel_id=1, source_target_pairs={{0,4},{4,0},{8,12},{12,8},{16,20},{20,16},{24,28},{28,24},{1,5},{5... | collective-permute-start | bytes 491528 | tf_op jit(solution)/shard_map/ppermute | solution.py:289
  57.2 0.7 copy-start.5
  57.2 0.7 copy-start.6
  57.2 0.8 %copy-start.15 = (bf16[2,160,256]{2,1,0:T(8,128)(2,1)}, bf16[2,160,256]{2,1,0:T(8,128)(2,1)S(1)}, u32[]{:S(2)}) copy-start(bf16[2,160,256]{2,1,0:T(8,128)(2,1)S(1)} %collective-permute-done.7.refs_7_) | copy-start | bytes 491524
  57.2 0.8 %copy-start.16 = (bf16[2,160,256]{2,1,0:T(8,128)(2,1)}, bf16[2,160,256]{2,1,0:T(8,128)(2,1)S(1)}, u32[]{:S(2)}) copy-start(bf16[2,160,256]{2,1,0:T(8,128)(2,1)S(1)} %collective-permute-done.5.refs_5_) | copy-start | bytes 491524
  57.2 0.9 %copy-start.17 = (bf16[2,160,256]{2,1,0:T(8,128)(2,1)}, bf16[2,160,256]{2,1,0:T(8,128)(2,1)S(1)}, u32[]{:S(2)}) copy-start(bf16[2,160,256]{2,1,0:T(8,128)(2,1)S(1)} %collective-permute-done.3.refs_3_) | copy-start | bytes 491524
where the time goes:
time: 79.7 us; the launch traced here: 79.4 us
  waiting for transfers between devices  27.3 us (34%)
  Pallas kernels  27.2 us (34%)
  starting transfers between devices  22 us (28%)
  local copies, waits for them, and re-layouts  2.02 us (3%)
  between operations  0.86 us (1%)
    pallas_call x1, Pallas kernels, whole(): pl.pallas_call(functools.partial(tile_kernel, n_row, n_col, columns, shar...  21.3 us
    ppermute x6, waiting for transfers between devices, along(): found.append(lax.ppermute(value, 'col', pairs))  21.2 us
    ppermute x6, starting transfers between devices, along(): found.append(lax.ppermute(value, 'col', pairs))  12.9 us
    ppermute x14, starting transfers between devices, flip(): return lax.ppermute(value, 'row', [(i, i ^ mask) for i in range(n_row)])  7.58 us
    ppermute x14, waiting for transfers between devices, flip(): return lax.ppermute(value, 'row', [(i, i ^ mask) for i in range(n_row)])  6.03 us
    pallas_call x1, Pallas kernels, whole(): pl.pallas_call(functools.partial(small_kernel, columns), out_shape=jax.Sh...  2.38 us
    unnamed x42, local copies, waits for them, and re-layouts  2.02 us
    pallas_call x1, Pallas kernels, whole(): pl.pallas_call(functools.partial(pack_kernel, shares), out_shape=(pair, p...  1.99 us
  transfers between devices with their start and end apart: 21, of which 5 were waited for; matrix products, arithmetic and copies ran while one was open for 0% of the time, Pallas kernels for 5%

commit v1 on v0

v1 whole, which is shorter than its diff:
```python
import functools
import math

import jax
import jax.numpy as jnp
from jax import lax
from jax.experimental import pallas as pl
from jax.experimental.pallas import tpu as pltpu
from jax.sharding import PartitionSpec as P


F32 = jnp.float32
BF16 = jnp.bfloat16
HIGH = lax.Precision.HIGHEST
GROUP = 8
SHARE_ROWS = 32
OUT_LANES = 256
VMEM = pl.BlockSpec(memory_space=pltpu.VMEM)
SMEM = pl.BlockSpec(memory_space=pltpu.SMEM)
HBM = pl.BlockSpec(memory_space=pltpu.HBM)
MIB = 1024 * 1024
LIGHT = pltpu.CompilerParams(vmem_limit_bytes=6 * MIB)

NN = ((1,), (0,))
NT = ((1,), (1,))


def contract(a, b, dims, precision=None):
    return lax.dot_general(
        a, b, (dims, ((), ())), preferred_element_type=F32, precision=precision
    )


def stacked(value, count):
    found = []
    for _ in range(count - 1):
        found.append(value.astype(BF16))
        value = value - found[-1].astype(F32)
    return jnp.concatenate(found + [value.astype(BF16)], axis=0)


def folded(value, count):
    size = value.shape[0] // count
    total = value[(count - 1) * size :]
    for index in range(count - 2, -1, -1):
        total = value[index * size : (index + 1) * size] + total
    return total


def below(width, rank, axis):
    shape = (width, 1) if axis == 0 else (1, width)
    return (lax.broadcasted_iota(jnp.int32, shape, axis) < rank).astype(F32)


def pack_kernel(shares, rank_ref, u_hbm, v_hbm, inverse_hbm, far_ref, near_ref, share_ref, v_ref, sem):
    rows, width = share_ref.shape[0], v_ref.shape[1]
    start = lax.rem(lax.axis_index("row"), shares) * rows
    part = inverse_hbm.at[pl.ds(pl.multiple_of(start, rows), rows), :]
    copies = [
        pltpu.make_async_copy(v_hbm.at[:, 0], v_ref, sem.at[0]),
        pltpu.make_async_copy(part, share_ref, sem.at[1]),
        pltpu.make_async_copy(u_hbm.at[0, 0], far_ref.at[0], sem.at[2]),
        pltpu.make_async_copy(u_hbm.at[1, 0], near_ref.at[0], sem.at[3]),
    ]
    for copy in copies:
        copy.start()
    copies[0].wait()
    for tile, out_ref in enumerate((far_ref, near_ref)):
        keep = below(width, rank_ref[0, tile], 0)
        out_ref[1] = (v_ref[tile].astype(F32) * keep).astype(BF16)
    for copy in copies[1:]:
        copy.wait()


def join_kernel(*refs):
    for index, ref in enumerate(refs[:-1]):
        refs[-1][index] = ref[...]


def eliminate(blocks):
    size = blocks[0].shape[0]
    count = size // GROUP
    unit = (
        lax.broadcasted_iota(jnp.int32, (size, size), 1)
        == lax.broadcasted_iota(jnp.int32, (size, size), 0)
    ).astype(F32)
    shape = (GROUP, 2 * size)
    sub = lax.broadcasted_iota(jnp.int32, shape, 0)
    held = []
    for block in blocks:
        both = jnp.concatenate([block, unit], axis=1)
        held.append([both[g * GROUP : (g + 1) * GROUP] for g in range(count)])

    def row_of(value, index):
        return jnp.broadcast_to(value[index : index + 1, :], shape)

    for g in range(count):
        for rows in held:
            columns = []
            for j in range(GROUP):
                spot = g * GROUP + j
                columns.append(
                    [jnp.broadcast_to(rows[h][:, spot : spot + 1], shape) for h in range(g, count)]
                )
            roots = []
            for j in range(GROUP):
                root = lax.rsqrt(row_of(columns[j][0], j))
                scaled = [value * root for value in columns[j]]
                scaled[0] = jnp.where(sub > j, scaled[0], 0.0)
                columns[j] = scaled
                roots.append(root)
                for k in range(j + 1, GROUP):
                    weight = row_of(scaled[0], k)
                    columns[k] = [a - b * weight for a, b in zip(columns[k], scaled)]
            top = rows[g]
            done = []
            for j in range(GROUP):
                row = row_of(top, j) * roots[j]
                done.append(row)
                top = jnp.where(sub == j, row, top - columns[j][0] * row)
            rows[g] = top
            for h in range(g + 1, count):
                for j in range(GROUP):
                    rows[h] = rows[h] - columns[j][h - g] * done[j]
    return [jnp.concatenate(rows, axis=0)[:, size:] for rows in held]


def block_sizes(width):
    sizes = []
    while width > 0:
        sizes.append(min(64, width))
        width -= sizes[-1]
    return sizes


def inverse_factors(grams, fillers):
    width = grams[0].shape[0]
    unit = (
        lax.broadcasted_iota(jnp.int32, (width, width), 0)
        == lax.broadcasted_iota(jnp.int32, (width, width), 1)
    ).astype(F32)
    rests = list(grams)
    sides = [unit for _ in grams]
    found = [[] for _ in grams]
    for turn, size in enumerate(block_sizes(width)):
        if turn < len(fillers):
            fillers[turn]()
        smalls = eliminate([rest[:size, :size] for rest in rests])
        for index, small in enumerate(smalls):
            rest, side = rests[index], sides[index]
            right = contract(small, side[:size], NN, HIGH)
            found[index].append(right)
            if rest.shape[0] > size:
                down = contract(rest[size:, :size], small, NT, HIGH)
                across = contract(small, rest[:size, size:], NN, HIGH)
                rests[index] = rest[size:, size:] - contract(down, across, NN, HIGH)
                sides[index] = side[size:] - contract(down, right, NN, HIGH)
    return [jnp.concatenate(rows, axis=0) for rows in found]


def six(left, right, dims):
    size, other = left.shape[0] // 3, right.shape[0] // 3
    first = contract(left, right[:other], dims)
    second = contract(left[: 2 * size], right[other : 2 * other], dims)
    third = contract(left[:size], right[2 * other :], dims)
    small = (first[2 * size :] + second[size:]) + third
    return first[:size] + ((first[size : 2 * size] + second[:size]) + small)


def three(left, right, dims):
    size, other = left.shape[0] // 2, right.shape[0] // 3
    first = contract(left, right[:other], dims)
    return first[:size] + (first[size:] + contract(left[:size], right[other : 2 * other], dims))


def spread_place(value, n_col):
    return value % 2 * (n_col // 2) + value // 2


def gather_place(value, n_col):
    return lax.rem(value, n_col // 2) * 2 + lax.div(value, n_col // 2)


def tile_kernel(n_row, n_col, columns, shares, rank_ref, *refs):
    (u_ref, v_hbm, w_hbm, inverse_ref), refs = refs[:4], refs[4:]
    far, near, refs = refs[:n_row], refs[n_row : n_row + n_col], refs[n_row + n_col :]
    pieces, refs = refs[:shares], refs[shares:]
    new_u_hbm, new_v_hbm, far_ref, near_ref, full, parts_ref, *refs = refs
    new_u_ref, new_v_ref, v_ref, w_ref, out_sem, in_sem = refs
    here = (lax.axis_index("row"), lax.axis_index("col"))

    def begin(copies):
        for copy in copies:
            copy.start()
        return copies

    def end(copies):
        for copy in copies:
            copy.wait()

    loads = begin(
        [
            pltpu.make_async_copy(v_hbm, v_ref, in_sem.at[0]),
            pltpu.make_async_copy(w_hbm, w_ref, in_sem.at[1]),
        ]
    )
    full[:, 0] = inverse_ref[...]
    for flip in range(shares):
        spot = lax.rem(lax.bitwise_xor(here[0], flip), shares)
        full[spot, 1:] = pieces[flip][...]
    for flip in range(n_row):
        source = lax.bitwise_xor(here[0], flip)
        chunk_of = lax.bitwise_xor(gather_place(lax.rem(source, n_col), n_col), here[1])
        far_ref[lax.div(source, n_col), chunk_of] = far[flip][...]
    for shift in range(n_col):
        near_ref[lax.bitwise_xor(here[1], shift)] = near[shift][...]
    width, height = u_ref.shape[3:]
    chunk = height // n_col
    spans = [slice(a * chunk, (a + 1) * chunk) for a in range(n_col)]
    eye = lax.broadcasted_iota(jnp.int32, (width, width), 0) == lax.broadcasted_iota(
        jnp.int32, (width, width), 1
    )
    across = [below(width, rank_ref[0, 0, c], 1) for c in range(columns)]

    def joined(index, c=None):
        if c is None:
            return jnp.concatenate([near_ref[a, index] for a in range(n_col)], axis=1)
        return jnp.concatenate([far_ref[c, a, index] for a in range(n_col)], axis=1)

    right = jnp.concatenate([joined(1, c) for c in range(columns)] + [joined(1)], axis=0)
    solved = []
    for a in range(n_col):
        last = (a + 1) * chunk
        shift = lax.bitwise_xor(here[1], a)
        piece = jnp.concatenate([full[share, shift] for share in range(shares)], axis=0)
        solved.append(contract(right[:, :last], piece[:, :last], NT).astype(BF16))
    solved = jnp.concatenate(solved, axis=1)
    couplings = [
        contract(solved[columns * width :], solved[c * width : (c + 1) * width], NT)
        for c in range(columns)
    ]
    end(loads)
    far_u = [joined(0, c) for c in range(columns)]
    near_u = joined(0)
    far_parts = []
    for c in range(columns):
        right = contract(w_ref[c, 0, 0], far_u[c], NT) * below(width, rank_ref[0, 0, c], 0)
        far_parts.append(stacked(-contract(right, couplings[c], NT, HIGH), 2))
    own_parts = []
    for c in range(columns):
        rank = rank_ref[0, 0, c]
        value = contract(w_ref[c, 0, 0], v_ref[c, 0, 0], NT)
        own_parts.append(stacked(value * below(width, rank, 0) * across[c], 2))
    for c in range(columns):
        for a in range(n_col):
            y = folded(
                contract(own_parts[c], u_ref[c, 0, 0, :, spans[a]], NN)
                + contract(far_parts[c], near_ref[a, 0], NN),
                2,
            )
            parts_ref[c, a] = stacked(y, 3)
    grams = []
    for c in range(columns):
        y = jnp.concatenate([parts_ref[c, a] for a in range(n_col)], axis=1)
        grams.append(six(y, y, NT) + jnp.where(eye, 1.0 - across[c], 0.0))
    own, far = [None] * columns, [None] * columns

    def project(c):
        y = jnp.concatenate([parts_ref[c, a] for a in range(n_col)], axis=1)
        own[c] = folded(contract(y, u_ref[c, 0, 0], NT), 3) * across[c]
        far[c] = folded(contract(y, near_u, NT), 3)

    inverses = inverse_factors(grams, [functools.partial(project, c) for c in range(columns)])
    factor = math.sqrt(height)
    sides = []
    for c in range(columns):
        scaled = inverses[c] * (1.0 / factor)
        left = contract(scaled, own[c], NN, HIGH)
        right = contract(contract(scaled, -far[c], NN, HIGH), couplings[c], NN, HIGH)
        sides.append((stacked(left, 2), stacked(right, 2)))
    outs = []
    reach = max(1, OUT_LANES // chunk)

    def send(index, c, a, room, target):
        if (a + 1) % reach == 0:
            lanes = slice((a + 1 - reach) * chunk, (a + 1) * chunk)
            spot = (c, 0, 0, slice(None), lanes)
            copy = pltpu.make_async_copy(room.at[spot], target.at[spot], out_sem.at[index, c, a])
            outs.extend(begin([copy]))

    for c in range(columns):
        scaled = stacked(inverses[c] * factor, 2)
        for a in range(n_col):
            new_u_ref[c, 0, 0, :, spans[a]] = three(scaled, parts_ref[c, a], NN)
            send(0, c, a, new_u_ref, new_u_hbm)
    for c in range(columns):
        left, right = sides[c]
        for a in range(n_col):
            new_v_ref[c, 0, 0, :, spans[a]] = folded(
                contract(left, v_ref[c, 0, 0, :, spans[a]], NN)
                + contract(right, far_ref[c, a, 0], NN),
                2,
            )
            send(1, c, a, new_v_ref, new_v_hbm)
    end(outs)


def in_hbm(value):
    return pltpu.with_memory_space_constraint(value, pltpu.HBM)


def share_count(n_row, chunk):
    return max(1, min(n_row, chunk // SHARE_ROWS))


def whole(panel_u, panel_v, panel_rank, diag_inverse, tile_u, tile_v, tile_rank, sketch):
    n_row, n_col = lax.axis_size("row"), lax.axis_size("col")
    panel_u, panel_v, tile_u, tile_v, sketch = (
        jnp.swapaxes(value, -1, -2) for value in (panel_u, panel_v, tile_u, tile_v, sketch)
    )
    panel_rank, tile_rank = jnp.swapaxes(panel_rank, 0, 1), jnp.moveaxis(tile_rank, 0, -1)
    width, chunk = panel_u.shape[2:]
    columns = tile_u.shape[0]
    pair = jax.ShapeDtypeStruct((2, width, chunk), BF16)

    def across(value):
        pairs = []
        for row in range(n_row):
            for col in range(n_col):
                spot = spread_place(row % n_col ^ col, n_col)
                pairs.append((row * n_col + col, (row // n_col * n_col + spot) * n_col + row % n_col))
        return lax.ppermute(value, ("row", "col"), pairs)

    def flip(value, mask):
        return lax.ppermute(value, "row", [(i, i ^ mask) for i in range(n_row)])

    def plane(value, count):
        same = {0: value}
        for mask in range(2, count, 2):
            same[mask] = flip(value, mask)
        full = dict(same)
        for mask in range(0, count, 2):
            full[mask + 1] = flip(same[mask], 1)
        return [full[mask] for mask in range(count)]

    def along(value):
        found = [value]
        for shift in range(1, n_col):
            pairs = [(i, i ^ shift) for i in range(n_col)]
            found.append(lax.ppermute(value, "col", pairs))
        return found

    shares = share_count(n_row, chunk)
    part = jax.ShapeDtypeStruct((chunk // shares, diag_inverse.shape[1]), BF16)
    far, near, share = pl.pallas_call(
        functools.partial(pack_kernel, shares),
        out_shape=(pair, pair, part),
        in_specs=[SMEM] + [HBM] * 3,
        out_specs=(VMEM,) * 3,
        scratch_shapes=[
            pltpu.VMEM((2, width, chunk), BF16),
            pltpu.SemaphoreType.DMA((4,)),
        ],
        compiler_params=LIGHT,
        name="pack",
    )(*(in_hbm(value) for value in (panel_rank, panel_u, panel_v, diag_inverse)))
    far, shared = across(far), along(share)[1:]
    near, far = along(near), plane(far, n_row)
    joined = pl.pallas_call(
        join_kernel,
        out_shape=jax.ShapeDtypeStruct((n_col - 1,) + share.shape, BF16),
        in_specs=[VMEM] * (n_col - 1),
        out_specs=VMEM,
        compiler_params=LIGHT,
        name="join",
    )(*shared)
    pieces = plane(joined, shares)
    result = jax.ShapeDtypeStruct(tile_u.shape, F32)
    new_u, new_v = pl.pallas_call(
        functools.partial(tile_kernel, n_row, n_col, columns, shares),
        out_shape=(result, result),
        in_specs=[SMEM, VMEM, HBM, HBM] + [VMEM] * (1 + n_row + n_col + shares),
        out_specs=(HBM, HBM),
        scratch_shapes=[
            pltpu.VMEM((columns, n_col, 2, width, chunk), BF16),
            pltpu.VMEM((n_col, 2, width, chunk), BF16),
            pltpu.VMEM((shares, n_col) + share.shape, BF16),
            pltpu.VMEM((columns, n_col, 3 * width, chunk), BF16),
            *[pltpu.VMEM(tile_u.shape, F32)] * 2,
            *[pltpu.VMEM(tile_u.shape, BF16)] * 2,
            pltpu.SemaphoreType.DMA((2, columns, n_col)),
            pltpu.SemaphoreType.DMA((2,)),
        ],
        compiler_params=pltpu.CompilerParams(vmem_limit_bytes=22 * MIB),
        name="tiles",
    )(in_hbm(tile_rank), tile_u, in_hbm(tile_v), in_hbm(sketch), diag_inverse.reshape((shares,) + share.shape), *far, *near, *pieces)
    return jnp.swapaxes(new_u, -1, -2), jnp.swapaxes(new_v, -1, -2)


def solution(mesh):
    n_row, n_col = mesh.shape["row"], mesh.shape["col"]
    assert n_row % n_col == 0
    wide = P(None, "row", "col", None)
    tile = P(None, "row", "col", None, None)
    return jax.shard_map(
        whole,
        mesh=mesh,
        in_specs=(wide, wide, P(None, "row"), P("col", None), tile, tile, P(None, "row", "col"), tile),
        out_specs=(tile, tile),
        check_vma=False,
    )
```

time: 79.7 us -> 72.2 us (0.906)
  Pallas kernels: 27.2 us -> 17.3 us
  waiting for transfers between devices: 27.3 us -> 32.5 us
  local copies, waits for them, and re-layouts: 2.02 us -> 0.01 us
    pallas_call x1, Pallas kernels: 21.3 us -> 15.4 us  [whole(): pl.pallas_call(functools.partial(tile_kernel, n_row, n_col, columns, shar...]
    ppermute x14, waiting for transfers between devices: 6.03 us -> 9.6 us  [flip(): return lax.ppermute(value, 'row', [(i, i ^ mask) for i in range(n_row)])]
    pallas_call x1 -> x0, Pallas kernels: 2.38 us -> none  [whole(): pl.pallas_call(functools.partial(small_kernel, columns), out_shape=jax.Sh...]
    unnamed x42 -> x4, local copies, waits for them, and re-layouts: 2.02 us -> 0.01 us
    ppermute x6, waiting for transfers between devices: 21.2 us -> 22.9 us  [along(): found.append(lax.ppermute(value, 'col', pairs))]
    pallas_call x1, Pallas kernels: 1.6 us -> 0.01 us  [whole(): pl.pallas_call(join_kernel, out_shape=jax.ShapeDtypeStruct((n_col - 1,) +...]
    ppermute x6, starting transfers between devices: 12.9 us -> 13.8 us  [along(): found.append(lax.ppermute(value, 'col', pairs))]
    ppermute x1, starting transfers between devices: 1.56 us -> 0.66 us  [across(): return lax.ppermute(value, ('row', 'col'), pairs)]
  transfers between devices with their start and end apart: 21 -> 21, of which waited for: 5 -> 10; matrix products, arithmetic and copies ran while one was open for 0% -> 0% of each run, Pallas kernels for 5% -> 0%
where the time goes in v1:
time: 72.2 us; the launch traced here: 72 us
  waiting for transfers between devices  32.5 us (45%)
  starting transfers between devices  21.5 us (30%)
  Pallas kernels  17.3 us (24%)
    ppermute x6, waiting for transfers between devices, along(): found.append(lax.ppermute(value, 'col', pairs))  22.9 us
    pallas_call x1, Pallas kernels, whole(): pl.pallas_call(functools.partial(tile_kernel, n_row, n_col, columns, shar...  15.4 us
    ppermute x6, starting transfers between devices, along(): found.append(lax.ppermute(value, 'col', pairs))  13.8 us
    ppermute x14, waiting for transfers between devices, flip(): return lax.ppermute(value, 'row', [(i, i ^ mask) for i in range(n_row)])  9.6 us
    ppermute x14, starting transfers between devices, flip(): return lax.ppermute(value, 'row', [(i, i ^ mask) for i in range(n_row)])  7.05 us
    pallas_call x1, Pallas kernels, whole(): pl.pallas_call(functools.partial(pack_kernel, shares), out_shape=(pair, p...  1.87 us
  transfers between devices with their start and end apart: 21, of which 10 were waited for; matrix products, arithmetic and copies ran while one was open for 0% of the time, Pallas kernels for 0%

profile of v1, /device:TPU:0, one launch (start us, length us, event | category | flops | bytes accessed | tf_op | source)
XLA Modules:
  0.0 72.0 jit_solution(16173847726888952988)
XLA Ops:
  0.6 0.0 copy-start
  0.6 0.0 copy-start.1
  0.7 1.9 %pack.1 = (bf16[2,160,256]{2,1,0:T(8,128)(2,1)S(1)}, bf16[2,160,256]{2,1,0:T(8,128)(2,1)S(1)}, bf16[32,1024]{1,0:T(8,128)(2,1)S(1)}) custom-call(s32[1,2]{1,0:T(1,128)} %bitcast.16, bf16[2,1,160,256]{3,2,1,0:T(8,128)(2,1)} %bitcast.14, bf16[2,1,160,256]{3,2,1,0:T(8,128)(2,1)} %bitcast.15, bf16[256,1024]{1,0:T(8,128)(2,1)} %inverse_hbm.1), custom_call_target="tpu_custom_call" | custom-call | tf_op jit(solution)/shard_map/pack/pallas_call | solution.py:355
  2.5 5.1 %collective-permute-start.13 = (bf16[32,1024]{1,0:T(8,128)(2,1)S(1)}, bf16[32,1024]{1,0:T(8,128)(2,1)S(1)}, u32[]{:S(2)}, u32[]{:S(2)}) collective-permute-start(bf16[32,1024]{1,0:T(8,128)(2,1)S(1)} %get-tuple-element.9), channel_id=1, source_target_pairs={{0,3},{1,2},{2,1},{3,0},{4,7},{5,6},{6,5},{7,4},{8,11},{9,10},{10,... | collective-permute-start | bytes 196616 | tf_op jit(solution)/shard_map/ppermute | solution.py:350
  7.7 0.7 collective-permute-start
  8.3 5.2 %collective-permute-start.10 = (bf16[2,160,256]{2,1,0:T(8,128)(2,1)S(1)}, bf16[2,160,256]{2,1,0:T(8,128)(2,1)S(1)}, u32[]{:S(2)}, u32[]{:S(2)}) collective-permute-start(bf16[2,160,256]{2,1,0:T(8,128)(2,1)S(1)} %get-tuple-element.8.refs_12_), channel_id=1, source_target_pairs={{0,3},{1,2},{2,1},{3,0},{4,7},{5,6},{6,5},{7,4},{8,11},{9,10},{10,... | collective-permute-start | bytes 491528 | tf_op jit(solution)/shard_map/ppermute | solution.py:350
  13.6 0.5 collective-permute-start.9
  14.1 2.4 %collective-permute-start.12 = (bf16[32,1024]{1,0:T(8,128)(2,1)S(1)}, bf16[32,1024]{1,0:T(8,128)(2,1)S(1)}, u32[]{:S(2)}, u32[]{:S(2)}) collective-permute-start(bf16[32,1024]{1,0:T(8,128)(2,1)S(1)} %get-tuple-element.9), channel_id=1, source_target_pairs={{0,2},{1,3},{2,0},{3,1},{4,6},{5,7},{6,4},{7,5},{8,10},{9,11},{10,... | collective-permute-start | bytes 196616 | tf_op jit(solution)/shard_map/ppermute | solution.py:350
  16.5 0.0 collective-permute-done.13.refs_2_
  16.5 0.0 collective-permute-start.11
  16.5 19.0 %collective-permute-done.12.refs_1_ = bf16[32,1024]{1,0:T(8,128)(2,1)S(1)} collective-permute-done((bf16[32,1024]{1,0:T(8,128)(2,1)S(1)}, bf16[32,1024]{1,0:T(8,128)(2,1)S(1)}, u32[]{:S(2)}, u32[]{:S(2)}) %collective-permute-start.12) | collective-permute-done | bytes 65568 | tf_op jit(solution)/shard_map/ppermute | solution.py:350
  35.5 0.0 collective-permute-done.11.refs_0_
  35.5 0.1 collective-permute-start.19
  35.6 1.6 %collective-permute-start.17 = (bf16[3,32,1024]{2,1,0:T(8,128)(2,1)S(1)}, bf16[3,32,1024]{2,1,0:T(8,128)(2,1)S(1)}, u32[]{:S(2)}, u32[]{:S(2)}) collective-permute-start(bf16[3,32,1024]{2,1,0:T(8,128)(2,1)S(1)} %join.1.refs_16_), channel_id=1, source_target_pairs={{0,16},{4,20},{8,24},{12,28},{16,0},{20,4},{24,8},{28,12},{1,17},{... | collective-permute-start | bytes 589832 | tf_op jit(solution)/shard_map/ppermute | solution.py:335
  37.2 0.0 collective-permute-done.refs_4_
  37.2 0.5 collective-permute-start.8
  37.7 0.0 collective-permute-done.10.refs_15_
  37.7 1.4 %collective-permute-start.15 = (bf16[3,32,1024]{2,1,0:T(8,128)(2,1)S(1)}, bf16[3,32,1024]{2,1,0:T(8,128)(2,1)S(1)}, u32[]{:S(2)}, u32[]{:S(2)}) collective-permute-start(bf16[3,32,1024]{2,1,0:T(8,128)(2,1)S(1)} %join.1.refs_16_), channel_id=1, source_target_pairs={{0,8},{4,12},{8,0},{12,4},{16,24},{20,28},{24,16},{28,20},{1,9},{5... | collective-permute-start | bytes 589832 | tf_op jit(solution)/shard_map/ppermute | solution.py:335
  39.1 0.0 collective-permute-done.9.refs_14_
  39.1 0.0 collective-permute-start.14
  39.1 3.9 %collective-permute-done.8.refs_13_ = bf16[2,160,256]{2,1,0:T(8,128)(2,1)S(1)} collective-permute-done((bf16[2,160,256]{2,1,0:T(8,128)(2,1)S(1)}, bf16[2,160,256]{2,1,0:T(8,128)(2,1)S(1)}, u32[]{:S(2)}, u32[]{:S(2)}) %collective-permute-start.8) | collective-permute-done | bytes 163872 | tf_op jit(solution)/shard_map/ppermute | solution.py:350
  43.0 2.6 %collective-permute-start.6 = (bf16[2,160,256]{2,1,0:T(8,128)(2,1)S(1)}, bf16[2,160,256]{2,1,0:T(8,128)(2,1)S(1)}, u32[]{:S(2)}, u32[]{:S(2)}) collective-permute-start(bf16[2,160,256]{2,1,0:T(8,128)(2,1)S(1)} %collective-permute-done.refs_4_), channel_id=1, source_target_pairs={{0,24},{4,28},{8,16},{12,20},{16,8},{20,12},{24,0},{28,4},{1,25},{... | collective-permute-start | bytes 491528 | tf_op jit(solution)/shard_map/ppermute | solution.py:335
  45.6 0.0 collective-permute-done.19.refs_22_
  45.6 0.5 collective-permute-start.4
  46.1 1.1 %collective-permute-done.17.refs_20_ = bf16[3,32,1024]{2,1,0:T(8,128)(2,1)S(1)} collective-permute-done((bf16[3,32,1024]{2,1,0:T(8,128)(2,1)S(1)}, bf16[3,32,1024]{2,1,0:T(8,128)(2,1)S(1)}, u32[]{:S(2)}, u32[]{:S(2)}) %collective-permute-start.17) | collective-permute-done | bytes 196640 | tf_op jit(solution)/shard_map/ppermute | solution.py:335
  47.1 0.0 collective-permute-start.20
  47.1 1.4 %collective-permute-done.15.refs_18_ = bf16[3,32,1024]{2,1,0:T(8,128)(2,1)S(1)} collective-permute-done((bf16[3,32,1024]{2,1,0:T(8,128)(2,1)S(1)}, bf16[3,32,1024]{2,1,0:T(8,128)(2,1)S(1)}, u32[]{:S(2)}, u32[]{:S(2)}) %collective-permute-start.15) | collective-permute-done | bytes 196640 | tf_op jit(solution)/shard_map/ppermute | solution.py:335
  48.5 0.1 collective-permute-start.2
  48.6 0.0 collective-permute-done.14.refs_17_
  48.6 0.2 collective-permute-start.1
  48.8 2.3 %collective-permute-done.6.refs_10_ = bf16[2,160,256]{2,1,0:T(8,128)(2,1)S(1)} collective-permute-done((bf16[2,160,256]{2,1,0:T(8,128)(2,1)S(1)}, bf16[2,160,256]{2,1,0:T(8,128)(2,1)S(1)}, u32[]{:S(2)}, u32[]{:S(2)}) %collective-permute-start.6) | collective-permute-done | bytes 163872 | tf_op jit(solution)/shard_map/ppermute | solution.py:335
  51.1 0.0 collective-permute-start.18
  51.1 2.5 %collective-permute-done.4.refs_8_ = bf16[2,160,256]{2,1,0:T(8,128)(2,1)S(1)} collective-permute-done((bf16[2,160,256]{2,1,0:T(8,128)(2,1)S(1)}, bf16[2,160,256]{2,1,0:T(8,128)(2,1)S(1)}, u32[]{:S(2)}, u32[]{:S(2)}) %collective-permute-start.4) | collective-permute-done | bytes 163872 | tf_op jit(solution)/shard_map/ppermute | solution.py:335
  53.7 0.0 collective-permute-start.16
  53.7 1.0 %collective-permute-done.2.refs_6_ = bf16[2,160,256]{2,1,0:T(8,128)(2,1)S(1)} collective-permute-done((bf16[2,160,256]{2,1,0:T(8,128)(2,1)S(1)}, bf16[2,160,256]{2,1,0:T(8,128)(2,1)S(1)}, u32[]{:S(2)}, u32[]{:S(2)}) %collective-permute-start.2) | collective-permute-done | bytes 163872 | tf_op jit(solution)/shard_map/ppermute | solution.py:335
  54.7 0.0 collective-permute-start.7
  54.7 0.0 collective-permute-done.1.refs_5_
  54.7 0.5 collective-permute-start.5
  55.2 0.0 collective-permute-done.20.refs_23_
  55.2 0.1 collective-permute-start.3
  55.2 0.0 collective-permute-done.18.refs_21_
  55.3 0.0 collective-permute-done.16.refs_19_
  55.3 0.8 %collective-permute-done.7.refs_11_ = bf16[2,160,256]{2,1,0:T(8,128)(2,1)S(1)} collective-permute-done((bf16[2,160,256]{2,1,0:T(8,128)(2,1)S(1)}, bf16[2,160,256]{2,1,0:T(8,128)(2,1)S(1)}, u32[]{:S(2)}, u32[]{:S(2)}) %collective-permute-start.7) | collective-permute-done | bytes 163872 | tf_op jit(solution)/shard_map/ppermute | solution.py:335
  56.1 0.2 collective-permute-done.5.refs_9_
  56.3 0.3 collective-permute-done.3.refs_7_
  56.6 0.0 copy-done
  56.6 0.0 copy-done.1
  56.6 15.4 %tiles.1 = (f32[2,1,1,160,1024]{4,3,2,1,0:T(8,128)}, f32[2,1,1,160,1024]{4,3,2,1,0:T(8,128)}) custom-call(s32[1,1,2]{2,1,0:T(1,128)} %bitcast.17, bf16[2,1,1,160,1024]{4,3,2,1,0:T(8,128)(2,1)S(1)} %bitcast.11, bf16[2,1,1,160,1024]{4,3,2,1,0:T(8,128)(2,1)} %bitcast.12, bf16[2,1,1,160,1024]{4,3,2,1,0:T(8,128)(2,1)} %bitcast.13, ...), custom_call_target="tpu_custom_call" | custom-call | tf_op jit(solution)/shard_map/tiles/pallas_call | solution.py:379
  (1 shorter events, 0.0 us)
Async XLA Ops:
  0.6 55.9 %copy-start = (bf16[256,1024]{1,0:T(8,128)(2,1)S(1)}, bf16[256,1024]{1,0:T(8,128)(2,1)}, u32[]{:S(2)}) copy-start(bf16[256,1024]{1,0:T(8,128)(2,1)} %inverse_hbm.1) | copy-start | bytes 1572868
  0.6 55.9 %copy-start.1 = (bf16[2,1,1,1024,160]{3,4,2,1,0:T(8,128)(2,1)S(1)}, bf16[2,1,1,1024,160]{3,4,2,1,0:T(8,128)(2,1)}, u32[]{:S(2)}) copy-start(bf16[2,1,1,1024,160]{3,4,2,1,0:T(8,128)(2,1)} %param.12) | copy-start | bytes 1966084
  2.5 14.0 %collective-permute-start.13 = (bf16[32,1024]{1,0:T(8,128)(2,1)S(1)}, bf16[32,1024]{1,0:T(8,128)(2,1)S(1)}, u32[]{:S(2)}, u32[]{:S(2)}) collective-permute-start(bf16[32,1024]{1,0:T(8,128)(2,1)S(1)} %get-tuple-element.9), channel_id=1, source_target_pairs={{0,3},{1,2},{2,1},{3,0},{4,7},{5,6},{6,5},{7,4},{8,11},{9,10},{10,... | collective-permute-start | bytes 196616 | tf_op jit(solution)/shard_map/ppermute | solution.py:350
  7.7 29.5 %collective-permute-start = (bf16[2,160,256]{2,1,0:T(8,128)(2,1)S(1)}, bf16[2,160,256]{2,1,0:T(8,128)(2,1)S(1)}, u32[]{:S(2)}, u32[]{:S(2)}) collective-permute-start(bf16[2,160,256]{2,1,0:T(8,128)(2,1)S(1)} %get-tuple-element.7), channel_id=1, source_target_pairs={{0,0},{1,8},{2,4},{3,12},{4,9},{5,1},{6,13},{7,5},{8,6},{9,14},{10... | collective-permute-start | bytes 491528 | tf_op jit(solution)/shard_map/ppermute | solution.py:332
  8.3 29.3 %collective-permute-start.10 = (bf16[2,160,256]{2,1,0:T(8,128)(2,1)S(1)}, bf16[2,160,256]{2,1,0:T(8,128)(2,1)S(1)}, u32[]{:S(2)}, u32[]{:S(2)}) collective-permute-start(bf16[2,160,256]{2,1,0:T(8,128)(2,1)S(1)} %get-tuple-element.8.refs_12_), channel_id=1, source_target_pairs={{0,3},{1,2},{2,1},{3,0},{4,7},{5,6},{6,5},{7,4},{8,11},{9,10},{10,... | collective-permute-start | bytes 491528 | tf_op jit(solution)/shard_map/ppermute | solution.py:350
  13.6 25.6 %collective-permute-start.9 = (bf16[2,160,256]{2,1,0:T(8,128)(2,1)S(1)}, bf16[2,160,256]{2,1,0:T(8,128)(2,1)S(1)}, u32[]{:S(2)}, u32[]{:S(2)}) collective-permute-start(bf16[2,160,256]{2,1,0:T(8,128)(2,1)S(1)} %get-tuple-element.8.refs_12_), channel_id=1, source_target_pairs={{0,2},{1,3},{2,0},{3,1},{4,6},{5,7},{6,4},{7,5},{8,10},{9,11},{10,... | collective-permute-start | bytes 491528 | tf_op jit(solution)/shard_map/ppermute | solution.py:350
  14.1 21.4 %collective-permute-start.12 = (bf16[32,1024]{1,0:T(8,128)(2,1)S(1)}, bf16[32,1024]{1,0:T(8,128)(2,1)S(1)}, u32[]{:S(2)}, u32[]{:S(2)}) collective-permute-start(bf16[32,1024]{1,0:T(8,128)(2,1)S(1)} %get-tuple-element.9), channel_id=1, source_target_pairs={{0,2},{1,3},{2,0},{3,1},{4,6},{5,7},{6,4},{7,5},{8,10},{9,11},{10,... | collective-permute-start | bytes 196616 | tf_op jit(solution)/shard_map/ppermute | solution.py:350
  16.5 19.0 %collective-permute-start.11 = (bf16[32,1024]{1,0:T(8,128)(2,1)S(1)}, bf16[32,1024]{1,0:T(8,128)(2,1)S(1)}, u32[]{:S(2)}, u32[]{:S(2)}) collective-permute-start(bf16[32,1024]{1,0:T(8,128)(2,1)S(1)} %get-tuple-element.9), channel_id=1, source_target_pairs={{0,1},{1,0},{2,3},{3,2},{4,5},{5,4},{6,7},{7,6},{8,9},{9,8},{10,11... | collective-permute-start | bytes 196616 | tf_op jit(solution)/shard_map/ppermute | solution.py:350
  35.5 10.1 %collective-permute-start.19 = (bf16[3,32,1024]{2,1,0:T(8,128)(2,1)S(1)}, bf16[3,32,1024]{2,1,0:T(8,128)(2,1)S(1)}, u32[]{:S(2)}, u32[]{:S(2)}) collective-permute-start(bf16[3,32,1024]{2,1,0:T(8,128)(2,1)S(1)} %join.1.refs_16_), channel_id=1, source_target_pairs={{0,24},{4,28},{8,16},{12,20},{16,8},{20,12},{24,0},{28,4},{1,25},{... | collective-permute-start | bytes 589832 | tf_op jit(solution)/shard_map/ppermute | solution.py:335
  35.6 11.6 %collective-permute-start.17 = (bf16[3,32,1024]{2,1,0:T(8,128)(2,1)S(1)}, bf16[3,32,1024]{2,1,0:T(8,128)(2,1)S(1)}, u32[]{:S(2)}, u32[]{:S(2)}) collective-permute-start(bf16[3,32,1024]{2,1,0:T(8,128)(2,1)S(1)} %join.1.refs_16_), channel_id=1, source_target_pairs={{0,16},{4,20},{8,24},{12,28},{16,0},{20,4},{24,8},{28,12},{1,17},{... | collective-permute-start | bytes 589832 | tf_op jit(solution)/shard_map/ppermute | solution.py:335
  37.2 5.8 %collective-permute-start.8 = (bf16[2,160,256]{2,1,0:T(8,128)(2,1)S(1)}, bf16[2,160,256]{2,1,0:T(8,128)(2,1)S(1)}, u32[]{:S(2)}, u32[]{:S(2)}) collective-permute-start(bf16[2,160,256]{2,1,0:T(8,128)(2,1)S(1)} %get-tuple-element.8.refs_12_), channel_id=1, source_target_pairs={{0,1},{1,0},{2,3},{3,2},{4,5},{5,4},{6,7},{7,6},{8,9},{9,8},{10,11... | collective-permute-start | bytes 491528 | tf_op jit(solution)/shard_map/ppermute | solution.py:350
  37.7 10.9 %collective-permute-start.15 = (bf16[3,32,1024]{2,1,0:T(8,128)(2,1)S(1)}, bf16[3,32,1024]{2,1,0:T(8,128)(2,1)S(1)}, u32[]{:S(2)}, u32[]{:S(2)}) collective-permute-start(bf16[3,32,1024]{2,1,0:T(8,128)(2,1)S(1)} %join.1.refs_16_), channel_id=1, source_target_pairs={{0,8},{4,12},{8,0},{12,4},{16,24},{20,28},{24,16},{28,20},{1,9},{5... | collective-permute-start | bytes 589832 | tf_op jit(solution)/shard_map/ppermute | solution.py:335
  39.1 9.5 %collective-permute-start.14 = (bf16[3,32,1024]{2,1,0:T(8,128)(2,1)S(1)}, bf16[3,32,1024]{2,1,0:T(8,128)(2,1)S(1)}, u32[]{:S(2)}, u32[]{:S(2)}) collective-permute-start(bf16[3,32,1024]{2,1,0:T(8,128)(2,1)S(1)} %join.1.refs_16_), channel_id=1, source_target_pairs={{0,4},{4,0},{8,12},{12,8},{16,20},{20,16},{24,28},{28,24},{1,5},{5... | collective-permute-start | bytes 589832 | tf_op jit(solution)/shard_map/ppermute | solution.py:335
  43.0 8.1 %collective-permute-start.6 = (bf16[2,160,256]{2,1,0:T(8,128)(2,1)S(1)}, bf16[2,160,256]{2,1,0:T(8,128)(2,1)S(1)}, u32[]{:S(2)}, u32[]{:S(2)}) collective-permute-start(bf16[2,160,256]{2,1,0:T(8,128)(2,1)S(1)} %collective-permute-done.refs_4_), channel_id=1, source_target_pairs={{0,24},{4,28},{8,16},{12,20},{16,8},{20,12},{24,0},{28,4},{1,25},{... | collective-permute-start | bytes 491528 | tf_op jit(solution)/shard_map/ppermute | solution.py:335
  45.6 8.1 %collective-permute-start.4 = (bf16[2,160,256]{2,1,0:T(8,128)(2,1)S(1)}, bf16[2,160,256]{2,1,0:T(8,128)(2,1)S(1)}, u32[]{:S(2)}, u32[]{:S(2)}) collective-permute-start(bf16[2,160,256]{2,1,0:T(8,128)(2,1)S(1)} %collective-permute-done.refs_4_), channel_id=1, source_target_pairs={{0,16},{4,20},{8,24},{12,28},{16,0},{20,4},{24,8},{28,12},{1,17},{... | collective-permute-start | bytes 491528 | tf_op jit(solution)/shard_map/ppermute | solution.py:335
  47.1 8.0 %collective-permute-start.20 = (bf16[3,32,1024]{2,1,0:T(8,128)(2,1)S(1)}, bf16[3,32,1024]{2,1,0:T(8,128)(2,1)S(1)}, u32[]{:S(2)}, u32[]{:S(2)}) collective-permute-start(bf16[3,32,1024]{2,1,0:T(8,128)(2,1)S(1)} %collective-permute-done.19.refs_22_), channel_id=1, source_target_pairs={{0,4},{4,0},{8,12},{12,8},{16,20},{20,16},{24,28},{28,24},{1,5},{5... | collective-permute-start | bytes 589832 | tf_op jit(solution)/shard_map/ppermute | solution.py:335
  48.5 6.1 %collective-permute-start.2 = (bf16[2,160,256]{2,1,0:T(8,128)(2,1)S(1)}, bf16[2,160,256]{2,1,0:T(8,128)(2,1)S(1)}, u32[]{:S(2)}, u32[]{:S(2)}) collective-permute-start(bf16[2,160,256]{2,1,0:T(8,128)(2,1)S(1)} %collective-permute-done.refs_4_), channel_id=1, source_target_pairs={{0,8},{4,12},{8,0},{12,4},{16,24},{20,28},{24,16},{28,20},{1,9},{5... | collective-permute-start | bytes 491528 | tf_op jit(solution)/shard_map/ppermute | solution.py:335
  48.6 6.0 %collective-permute-start.1 = (bf16[2,160,256]{2,1,0:T(8,128)(2,1)S(1)}, bf16[2,160,256]{2,1,0:T(8,128)(2,1)S(1)}, u32[]{:S(2)}, u32[]{:S(2)}) collective-permute-start(bf16[2,160,256]{2,1,0:T(8,128)(2,1)S(1)} %collective-permute-done.refs_4_), channel_id=1, source_target_pairs={{0,4},{4,0},{8,12},{12,8},{16,20},{20,16},{24,28},{28,24},{1,5},{5... | collective-permute-start | bytes 491528 | tf_op jit(solution)/shard_map/ppermute | solution.py:335
  51.1 4.1 %collective-permute-start.18 = (bf16[3,32,1024]{2,1,0:T(8,128)(2,1)S(1)}, bf16[3,32,1024]{2,1,0:T(8,128)(2,1)S(1)}, u32[]{:S(2)}, u32[]{:S(2)}) collective-permute-start(bf16[3,32,1024]{2,1,0:T(8,128)(2,1)S(1)} %collective-permute-done.17.refs_20_), channel_id=1, source_target_pairs={{0,4},{4,0},{8,12},{12,8},{16,20},{20,16},{24,28},{28,24},{1,5},{5... | collective-permute-start | bytes 589832 | tf_op jit(solution)/shard_map/ppermute | solution.py:335
  53.7 1.6 %collective-permute-start.16 = (bf16[3,32,1024]{2,1,0:T(8,128)(2,1)S(1)}, bf16[3,32,1024]{2,1,0:T(8,128)(2,1)S(1)}, u32[]{:S(2)}, u32[]{:S(2)}) collective-permute-start(bf16[3,32,1024]{2,1,0:T(8,128)(2,1)S(1)} %collective-permute-done.15.refs_18_), channel_id=1, source_target_pairs={{0,4},{4,0},{8,12},{12,8},{16,20},{20,16},{24,28},{28,24},{1,5},{5... | collective-permute-start | bytes 589832 | tf_op jit(solution)/shard_map/ppermute | solution.py:335
  54.7 1.4 %collective-permute-start.7 = (bf16[2,160,256]{2,1,0:T(8,128)(2,1)S(1)}, bf16[2,160,256]{2,1,0:T(8,128)(2,1)S(1)}, u32[]{:S(2)}, u32[]{:S(2)}) collective-permute-start(bf16[2,160,256]{2,1,0:T(8,128)(2,1)S(1)} %collective-permute-done.6.refs_10_), channel_id=1, source_target_pairs={{0,4},{4,0},{8,12},{12,8},{16,20},{20,16},{24,28},{28,24},{1,5},{5... | collective-permute-start | bytes 491528 | tf_op jit(solution)/shard_map/ppermute | solution.py:335
  54.7 1.6 %collective-permute-start.5 = (bf16[2,160,256]{2,1,0:T(8,128)(2,1)S(1)}, bf16[2,160,256]{2,1,0:T(8,128)(2,1)S(1)}, u32[]{:S(2)}, u32[]{:S(2)}) collective-permute-start(bf16[2,160,256]{2,1,0:T(8,128)(2,1)S(1)} %collective-permute-done.4.refs_8_), channel_id=1, source_target_pairs={{0,4},{4,0},{8,12},{12,8},{16,20},{20,16},{24,28},{28,24},{1,5},{5... | collective-permute-start | bytes 491528 | tf_op jit(solution)/shard_map/ppermute | solution.py:335
  55.2 1.4 %collective-permute-start.3 = (bf16[2,160,256]{2,1,0:T(8,128)(2,1)S(1)}, bf16[2,160,256]{2,1,0:T(8,128)(2,1)S(1)}, u32[]{:S(2)}, u32[]{:S(2)}) collective-permute-start(bf16[2,160,256]{2,1,0:T(8,128)(2,1)S(1)} %collective-permute-done.2.refs_6_), channel_id=1, source_target_pairs={{0,4},{4,0},{8,12},{12,8},{16,20},{20,16},{24,28},{28,24},{1,5},{5... | collective-permute-start | bytes 491528 | tf_op jit(solution)/shard_map/ppermute | solution.py:335

commit v2 on v1

--- a/solution.py
+++ b/solution.py
@@ -72,9 +72,38 @@
         copy.wait()
 
 
-def join_kernel(*refs):
-    for index, ref in enumerate(refs[:-1]):
-        refs[-1][index] = ref[...]
+def unit_width(chunk, height):
+    return chunk if chunk % 128 == 0 else height
+
+
+def piece_count(plane, packed):
+    return plane + 1 if packed else 1
+
+
+def piece_start(plane, here, packed):
+    before = sum(piece_count(other, packed) for other in range(plane))
+    own = here + 1 if packed else 1
+    return before - jnp.where(here < plane, own, 0)
+
+
+def piece_total(n_col, packed):
+    return sum(piece_count(plane, packed) for plane in range(1, n_col))
+
+
+def join_kernel(n_col, packed, *refs):
+    here = lax.axis_index("col")
+    out_ref = refs[-1]
+    unit = out_ref.shape[2]
+    for mask in range(1, n_col):
+        plane = lax.bitwise_xor(here, mask)
+        value = refs[mask - 1]
+        for source in range(n_col):
+
+            @pl.when(plane == source)
+            def _():
+                start = piece_start(source, here, packed)
+                for index in range(piece_count(source, packed)):
+                    out_ref[start + index] = value[:, index * unit : (index + 1) * unit]
 
 
 def eliminate(blocks):
@@ -181,7 +210,7 @@
     return lax.rem(value, n_col // 2) * 2 + lax.div(value, n_col // 2)
 
 
-def tile_kernel(n_row, n_col, columns, shares, rank_ref, *refs):
+def tile_kernel(n_row, n_col, columns, shares, packed, rank_ref, *refs):
     (u_ref, v_hbm, w_hbm, inverse_ref), refs = refs[:4], refs[4:]
     far, near, refs = refs[:n_row], refs[n_row : n_row + n_col], refs[n_row + n_col :]
     pieces, refs = refs[:shares], refs[shares:]
@@ -204,10 +233,24 @@
             pltpu.make_async_copy(w_hbm, w_ref, in_sem.at[1]),
         ]
     )
-    full[:, 0] = inverse_ref[...]
     for flip in range(shares):
         spot = lax.rem(lax.bitwise_xor(here[0], flip), shares)
-        full[spot, 1:] = pieces[flip][...]
+        unit = pieces[flip].shape[2]
+        for plane in range(n_col):
+            start = piece_start(plane, here[1], packed)
+            count = piece_count(plane, packed)
+
+            @pl.when(here[1] != plane)
+            def _():
+                for index in range(count):
+                    lanes = slice(index * unit, (index + 1) * unit)
+                    full[plane, spot, :, lanes] = pieces[flip][start + index]
+
+            @pl.when(here[1] == plane)
+            def _():
+                lanes = slice(0, count * unit)
+                full[plane, spot, :, lanes] = inverse_ref[spot, :, lanes]
+
     for flip in range(n_row):
         source = lax.bitwise_xor(here[0], flip)
         chunk_of = lax.bitwise_xor(gather_place(lax.rem(source, n_col), n_col), here[1])
@@ -231,8 +274,7 @@
     solved = []
     for a in range(n_col):
         last = (a + 1) * chunk
-        shift = lax.bitwise_xor(here[1], a)
-        piece = jnp.concatenate([full[share, shift] for share in range(shares)], axis=0)
+        piece = jnp.concatenate([full[a, share] for share in range(shares)], axis=0)
         solved.append(contract(right[:, :last], piece[:, :last], NT).astype(BF16))
     solved = jnp.concatenate(solved, axis=1)
     couplings = [
@@ -352,6 +394,9 @@
 
     shares = share_count(n_row, chunk)
     part = jax.ShapeDtypeStruct((chunk // shares, diag_inverse.shape[1]), BF16)
+    unit = unit_width(chunk, diag_inverse.shape[1])
+    packed = unit == chunk
+    total = piece_total(n_col, packed)
     far, near, share = pl.pallas_call(
         functools.partial(pack_kernel, shares),
         out_shape=(pair, pair, part),
@@ -367,8 +412,8 @@
     far, shared = across(far), along(share)[1:]
     near, far = along(near), plane(far, n_row)
     joined = pl.pallas_call(
-        join_kernel,
-        out_shape=jax.ShapeDtypeStruct((n_col - 1,) + share.shape, BF16),
+        functools.partial(join_kernel, n_col, packed),
+        out_shape=jax.ShapeDtypeStruct((total, share.shape[0], unit), BF16),
         in_specs=[VMEM] * (n_col - 1),
         out_specs=VMEM,
         compiler_params=LIGHT,
@@ -377,14 +422,14 @@
     pieces = plane(joined, shares)
     result = jax.ShapeDtypeStruct(tile_u.shape, F32)
     new_u, new_v = pl.pallas_call(
-        functools.partial(tile_kernel, n_row, n_col, columns, shares),
+        functools.partial(tile_kernel, n_row, n_col, columns, shares, packed),
         out_shape=(result, result),
         in_specs=[SMEM, VMEM, HBM, HBM] + [VMEM] * (1 + n_row + n_col + shares),
         out_specs=(HBM, HBM),
         scratch_shapes=[
             pltpu.VMEM((columns, n_col, 2, width, chunk), BF16),
             pltpu.VMEM((n_col, 2, width, chunk), BF16),
-            pltpu.VMEM((shares, n_col) + share.shape, BF16),
+            pltpu.VMEM((n_col, shares) + share.shape, BF16),
             pltpu.VMEM((columns, n_col, 3 * width, chunk), BF16),
             *[pltpu.VMEM(tile_u.shape, F32)] * 2,
             *[pltpu.VMEM(tile_u.shape, BF16)] * 2,

time: 72.2 us -> 73.1 us (1.012)
  starting transfers between devices: 21.5 us -> 31 us
  waiting for transfers between devices: 32.5 us -> 23.6 us
    ppermute x6, waiting for transfers between devices: 22.9 us -> 13.4 us  [along(): found.append(lax.ppermute(value, 'col', pairs))]
    ppermute x6, starting transfers between devices: 13.8 us -> 22.6 us  [along(): found.append(lax.ppermute(value, 'col', pairs))]
  transfers between devices with their start and end apart: 21 -> 21, of which waited for: 10 -> 11; matrix products, arithmetic and copies ran while one was open for 0% -> 0% of each run, Pallas kernels for 0% -> 0%
where the time goes in v2:
time: 73.1 us; the launch traced here: 72.9 us
  starting transfers between devices  31 us (42%)
  waiting for transfers between devices  23.6 us (32%)
  Pallas kernels  17.5 us (24%)
  between operations  0.88 us (1%)
    ppermute x6, starting transfers between devices, along(): found.append(lax.ppermute(value, 'col', pairs))  22.6 us
    pallas_call x1, Pallas kernels, whole(): pl.pallas_call(functools.partial(tile_kernel, n_row, n_col, columns, shar...  15.5 us
    ppermute x6, waiting for transfers between devices, along(): found.append(lax.ppermute(value, 'col', pairs))  13.4 us
    ppermute x14, waiting for transfers between devices, flip(): return lax.ppermute(value, 'row', [(i, i ^ mask) for i in range(n_row)])  10.2 us
    ppermute x14, starting transfers between devices, flip(): return lax.ppermute(value, 'row', [(i, i ^ mask) for i in range(n_row)])  7.74 us
    pallas_call x1, Pallas kernels, whole(): pl.pallas_call(functools.partial(pack_kernel, shares), out_shape=(pair, p...  1.87 us
  transfers between devices with their start and end apart: 21, of which 11 were waited for; matrix products, arithmetic and copies ran while one was open for 0% of the time, Pallas kernels for 0%

profile of v2, /device:TPU:0, one launch (start us, length us, event | category | flops | bytes accessed | tf_op | source)
XLA Modules:
  0.0 72.9 jit_solution(17795295425814057289)
XLA Ops:
  0.6 0.0 copy-start
  0.6 0.0 copy-start.1
  0.7 1.9 %pack.1 = (bf16[2,160,256]{2,1,0:T(8,128)(2,1)S(1)}, bf16[2,160,256]{2,1,0:T(8,128)(2,1)S(1)}, bf16[32,1024]{1,0:T(8,128)(2,1)S(1)}) custom-call(s32[1,2]{1,0:T(1,128)} %bitcast.16, bf16[2,1,160,256]{3,2,1,0:T(8,128)(2,1)} %bitcast.14, bf16[2,1,160,256]{3,2,1,0:T(8,128)(2,1)} %bitcast.15, bf16[256,1024]{1,0:T(8,128)(2,1)} %inverse_hbm.1), custom_call_target="tpu_custom_call" | custom-call | tf_op jit(solution)/shard_map/pack/pallas_call | solution.py:400
  2.5 0.7 collective-permute-start
  3.2 7.0 %collective-permute-start.10 = (bf16[2,160,256]{2,1,0:T(8,128)(2,1)S(1)}, bf16[2,160,256]{2,1,0:T(8,128)(2,1)S(1)}, u32[]{:S(2)}, u32[]{:S(2)}) collective-permute-start(bf16[2,160,256]{2,1,0:T(8,128)(2,1)S(1)} %get-tuple-element.8.refs_12_), channel_id=1, source_target_pairs={{0,3},{1,2},{2,1},{3,0},{4,7},{5,6},{6,5},{7,4},{8,11},{9,10},{10,... | collective-permute-start | bytes 491528 | tf_op jit(solution)/shard_map/ppermute | solution.py:392
  10.2 0.1 collective-permute-start.13
  10.3 0.4 collective-permute-start.9
  10.6 2.6 %collective-permute-start.12 = (bf16[32,1024]{1,0:T(8,128)(2,1)S(1)}, bf16[32,1024]{1,0:T(8,128)(2,1)S(1)}, u32[]{:S(2)}, u32[]{:S(2)}) collective-permute-start(bf16[32,1024]{1,0:T(8,128)(2,1)S(1)} %get-tuple-element.9), channel_id=1, source_target_pairs={{0,2},{1,3},{2,0},{3,1},{4,6},{5,7},{6,4},{7,5},{8,10},{9,11},{10,... | collective-permute-start | bytes 196616 | tf_op jit(solution)/shard_map/ppermute | solution.py:392
  13.2 6.4 %collective-permute-done.13.refs_2_ = bf16[32,1024]{1,0:T(8,128)(2,1)S(1)} collective-permute-done((bf16[32,1024]{1,0:T(8,128)(2,1)S(1)}, bf16[32,1024]{1,0:T(8,128)(2,1)S(1)}, u32[]{:S(2)}, u32[]{:S(2)}) %collective-permute-start.13) | collective-permute-done | bytes 65568 | tf_op jit(solution)/shard_map/ppermute | solution.py:392
  19.6 12.6 %collective-permute-start.11 = (bf16[32,1024]{1,0:T(8,128)(2,1)S(1)}, bf16[32,1024]{1,0:T(8,128)(2,1)S(1)}, u32[]{:S(2)}, u32[]{:S(2)}) collective-permute-start(bf16[32,1024]{1,0:T(8,128)(2,1)S(1)} %get-tuple-element.9), channel_id=1, source_target_pairs={{0,1},{1,0},{2,3},{3,2},{4,5},{5,4},{6,7},{7,6},{8,9},{9,8},{10,11... | collective-permute-start | bytes 196616 | tf_op jit(solution)/shard_map/ppermute | solution.py:392
  32.2 4.4 %collective-permute-done.12.refs_1_ = bf16[32,1024]{1,0:T(8,128)(2,1)S(1)} collective-permute-done((bf16[32,1024]{1,0:T(8,128)(2,1)S(1)}, bf16[32,1024]{1,0:T(8,128)(2,1)S(1)}, u32[]{:S(2)}, u32[]{:S(2)}) %collective-permute-start.12) | collective-permute-done | bytes 65568 | tf_op jit(solution)/shard_map/ppermute | solution.py:392
  36.6 0.0 collective-permute-start.8
  36.6 1.5 %collective-permute-done.11.refs_0_ = bf16[32,1024]{1,0:T(8,128)(2,1)S(1)} collective-permute-done((bf16[32,1024]{1,0:T(8,128)(2,1)S(1)}, bf16[32,1024]{1,0:T(8,128)(2,1)S(1)}, u32[]{:S(2)}, u32[]{:S(2)}) %collective-permute-start.11) | collective-permute-done | bytes 65568 | tf_op jit(solution)/shard_map/ppermute | solution.py:392
  38.2 0.3 collective-permute-start.19
  38.5 0.0 collective-permute-done.refs_4_
  38.5 1.4 %collective-permute-start.17 = (bf16[9,32,256]{2,1,0:T(8,128)(2,1)S(1)}, bf16[9,32,256]{2,1,0:T(8,128)(2,1)S(1)}, u32[]{:S(2)}, u32[]{:S(2)}) collective-permute-start(bf16[9,32,256]{2,1,0:T(8,128)(2,1)S(1)} %join.1.refs_16_), channel_id=1, source_target_pairs={{0,16},{4,20},{8,24},{12,28},{16,0},{20,4},{24,8},{28,12},{1,17},{... | collective-permute-start | bytes 442376 | tf_op jit(solution)/shard_map/ppermute | solution.py:377
  39.9 0.0 collective-permute-done.10.refs_15_
  39.9 1.9 %collective-permute-start.15 = (bf16[9,32,256]{2,1,0:T(8,128)(2,1)S(1)}, bf16[9,32,256]{2,1,0:T(8,128)(2,1)S(1)}, u32[]{:S(2)}, u32[]{:S(2)}) collective-permute-start(bf16[9,32,256]{2,1,0:T(8,128)(2,1)S(1)} %join.1.refs_16_), channel_id=1, source_target_pairs={{0,8},{4,12},{8,0},{12,4},{16,24},{20,28},{24,16},{28,20},{1,9},{5... | collective-permute-start | bytes 442376 | tf_op jit(solution)/shard_map/ppermute | solution.py:377
  41.7 0.0 collective-permute-done.9.refs_14_
  41.7 0.0 collective-permute-start.14
  41.7 1.0 %collective-permute-done.8.refs_13_ = bf16[2,160,256]{2,1,0:T(8,128)(2,1)S(1)} collective-permute-done((bf16[2,160,256]{2,1,0:T(8,128)(2,1)S(1)}, bf16[2,160,256]{2,1,0:T(8,128)(2,1)S(1)}, u32[]{:S(2)}, u32[]{:S(2)}) %collective-permute-start.8) | collective-permute-done | bytes 163872 | tf_op jit(solution)/shard_map/ppermute | solution.py:392
  42.8 0.5 collective-permute-start.6
  43.2 2.7 %collective-permute-done.19.refs_22_ = bf16[9,32,256]{2,1,0:T(8,128)(2,1)S(1)} collective-permute-done((bf16[9,32,256]{2,1,0:T(8,128)(2,1)S(1)}, bf16[9,32,256]{2,1,0:T(8,128)(2,1)S(1)}, u32[]{:S(2)}, u32[]{:S(2)}) %collective-permute-start.19) | collective-permute-done | bytes 147488 | tf_op jit(solution)/shard_map/ppermute | solution.py:377
  45.9 1.5 %collective-permute-start.4 = (bf16[2,160,256]{2,1,0:T(8,128)(2,1)S(1)}, bf16[2,160,256]{2,1,0:T(8,128)(2,1)S(1)}, u32[]{:S(2)}, u32[]{:S(2)}) collective-permute-start(bf16[2,160,256]{2,1,0:T(8,128)(2,1)S(1)} %collective-permute-done.refs_4_), channel_id=1, source_target_pairs={{0,16},{4,20},{8,24},{12,28},{16,0},{20,4},{24,8},{28,12},{1,17},{... | collective-permute-start | bytes 491528 | tf_op jit(solution)/shard_map/ppermute | solution.py:377
  47.4 1.0 %collective-permute-done.17.refs_20_ = bf16[9,32,256]{2,1,0:T(8,128)(2,1)S(1)} collective-permute-done((bf16[9,32,256]{2,1,0:T(8,128)(2,1)S(1)}, bf16[9,32,256]{2,1,0:T(8,128)(2,1)S(1)}, u32[]{:S(2)}, u32[]{:S(2)}) %collective-permute-start.17) | collective-permute-done | bytes 147488 | tf_op jit(solution)/shard_map/ppermute | solution.py:377
  48.4 1.1 %collective-permute-start.2 = (bf16[2,160,256]{2,1,0:T(8,128)(2,1)S(1)}, bf16[2,160,256]{2,1,0:T(8,128)(2,1)S(1)}, u32[]{:S(2)}, u32[]{:S(2)}) collective-permute-start(bf16[2,160,256]{2,1,0:T(8,128)(2,1)S(1)} %collective-permute-done.refs_4_), channel_id=1, source_target_pairs={{0,8},{4,12},{8,0},{12,4},{16,24},{20,28},{24,16},{28,20},{1,9},{5... | collective-permute-start | bytes 491528 | tf_op jit(solution)/shard_map/ppermute | solution.py:377
  49.5 0.0 collective-permute-done.15.refs_18_
  49.5 0.0 collective-permute-start.1
  49.5 0.0 collective-permute-done.14.refs_17_
  49.5 0.5 collective-permute-start.20
  50.0 2.6 %collective-permute-done.6.refs_10_ = bf16[2,160,256]{2,1,0:T(8,128)(2,1)S(1)} collective-permute-done((bf16[2,160,256]{2,1,0:T(8,128)(2,1)S(1)}, bf16[2,160,256]{2,1,0:T(8,128)(2,1)S(1)}, u32[]{:S(2)}, u32[]{:S(2)}) %collective-permute-start.6) | collective-permute-done | bytes 163872 | tf_op jit(solution)/shard_map/ppermute | solution.py:377
  52.6 0.0 collective-permute-start.7
  52.6 1.7 %collective-permute-done.4.refs_8_ = bf16[2,160,256]{2,1,0:T(8,128)(2,1)S(1)} collective-permute-done((bf16[2,160,256]{2,1,0:T(8,128)(2,1)S(1)}, bf16[2,160,256]{2,1,0:T(8,128)(2,1)S(1)}, u32[]{:S(2)}, u32[]{:S(2)}) %collective-permute-start.4) | collective-permute-done | bytes 163872 | tf_op jit(solution)/shard_map/ppermute | solution.py:377
  54.4 0.0 collective-permute-start.5
  54.4 0.9 %collective-permute-done.2.refs_6_ = bf16[2,160,256]{2,1,0:T(8,128)(2,1)S(1)} collective-permute-done((bf16[2,160,256]{2,1,0:T(8,128)(2,1)S(1)}, bf16[2,160,256]{2,1,0:T(8,128)(2,1)S(1)}, u32[]{:S(2)}, u32[]{:S(2)}) %collective-permute-start.2) | collective-permute-done | bytes 163872 | tf_op jit(solution)/shard_map/ppermute | solution.py:377
  55.3 0.0 collective-permute-start.3
  55.3 0.0 collective-permute-done.1.refs_5_
  55.3 0.5 collective-permute-start.18
  55.8 0.0 collective-permute-done.20.refs_23_
  55.8 0.1 collective-permute-start.16
  55.9 1.0 %collective-permute-done.18.refs_21_ = bf16[9,32,256]{2,1,0:T(8,128)(2,1)S(1)} collective-permute-done((bf16[9,32,256]{2,1,0:T(8,128)(2,1)S(1)}, bf16[9,32,256]{2,1,0:T(8,128)(2,1)S(1)}, u32[]{:S(2)}, u32[]{:S(2)}) %collective-permute-start.18) | collective-permute-done | bytes 147488 | tf_op jit(solution)/shard_map/ppermute | solution.py:377
  56.9 0.3 collective-permute-done.16.refs_19_
  57.2 0.0 collective-permute-done.7.refs_11_
  57.2 0.0 collective-permute-done.5.refs_9_
  57.2 0.0 collective-permute-done.3.refs_7_
  57.2 0.0 copy-done
  57.2 0.0 copy-done.1
  57.2 15.5 %tiles.1 = (f32[2,1,1,160,1024]{4,3,2,1,0:T(8,128)}, f32[2,1,1,160,1024]{4,3,2,1,0:T(8,128)}) custom-call(s32[1,1,2]{2,1,0:T(1,128)} %bitcast.17, bf16[2,1,1,160,1024]{4,3,2,1,0:T(8,128)(2,1)S(1)} %bitcast.11, bf16[2,1,1,160,1024]{4,3,2,1,0:T(8,128)(2,1)} %bitcast.12, bf16[2,1,1,160,1024]{4,3,2,1,0:T(8,128)(2,1)} %bitcast.13, ...), custom_call_target="tpu_custom_call" | custom-call | tf_op jit(solution)/shard_map/tiles/pallas_call | solution.py:424
  (1 shorter events, 0.0 us)
Async XLA Ops:
  0.6 56.6 %copy-start = (bf16[256,1024]{1,0:T(8,128)(2,1)S(1)}, bf16[256,1024]{1,0:T(8,128)(2,1)}, u32[]{:S(2)}) copy-start(bf16[256,1024]{1,0:T(8,128)(2,1)} %inverse_hbm.1) | copy-start | bytes 1572868
  0.6 56.6 %copy-start.1 = (bf16[2,1,1,1024,160]{3,4,2,1,0:T(8,128)(2,1)S(1)}, bf16[2,1,1,1024,160]{3,4,2,1,0:T(8,128)(2,1)}, u32[]{:S(2)}) copy-start(bf16[2,1,1,1024,160]{3,4,2,1,0:T(8,128)(2,1)} %param.12) | copy-start | bytes 1966084
  2.5 35.9 %collective-permute-start = (bf16[2,160,256]{2,1,0:T(8,128)(2,1)S(1)}, bf16[2,160,256]{2,1,0:T(8,128)(2,1)S(1)}, u32[]{:S(2)}, u32[]{:S(2)}) collective-permute-start(bf16[2,160,256]{2,1,0:T(8,128)(2,1)S(1)} %get-tuple-element.7), channel_id=1, source_target_pairs={{0,0},{1,8},{2,4},{3,12},{4,9},{5,1},{6,13},{7,5},{8,6},{9,14},{10... | collective-permute-start | bytes 491528 | tf_op jit(solution)/shard_map/ppermute | solution.py:374
  3.2 36.6 %collective-permute-start.10 = (bf16[2,160,256]{2,1,0:T(8,128)(2,1)S(1)}, bf16[2,160,256]{2,1,0:T(8,128)(2,1)S(1)}, u32[]{:S(2)}, u32[]{:S(2)}) collective-permute-start(bf16[2,160,256]{2,1,0:T(8,128)(2,1)S(1)} %get-tuple-element.8.refs_12_), channel_id=1, source_target_pairs={{0,3},{1,2},{2,1},{3,0},{4,7},{5,6},{6,5},{7,4},{8,11},{9,10},{10,... | collective-permute-start | bytes 491528 | tf_op jit(solution)/shard_map/ppermute | solution.py:392
  10.2 9.4 %collective-permute-start.13 = (bf16[32,1024]{1,0:T(8,128)(2,1)S(1)}, bf16[32,1024]{1,0:T(8,128)(2,1)S(1)}, u32[]{:S(2)}, u32[]{:S(2)}) collective-permute-start(bf16[32,1024]{1,0:T(8,128)(2,1)S(1)} %get-tuple-element.9), channel_id=1, source_target_pairs={{0,3},{1,2},{2,1},{3,0},{4,7},{5,6},{6,5},{7,4},{8,11},{9,10},{10,... | collective-permute-start | bytes 196616 | tf_op jit(solution)/shard_map/ppermute | solution.py:392
  10.3 31.5 %collective-permute-start.9 = (bf16[2,160,256]{2,1,0:T(8,128)(2,1)S(1)}, bf16[2,160,256]{2,1,0:T(8,128)(2,1)S(1)}, u32[]{:S(2)}, u32[]{:S(2)}) collective-permute-start(bf16[2,160,256]{2,1,0:T(8,128)(2,1)S(1)} %get-tuple-element.8.refs_12_), channel_id=1, source_target_pairs={{0,2},{1,3},{2,0},{3,1},{4,6},{5,7},{6,4},{7,5},{8,10},{9,11},{10,... | collective-permute-start | bytes 491528 | tf_op jit(solution)/shard_map/ppermute | solution.py:392
  10.6 26.0 %collective-permute-start.12 = (bf16[32,1024]{1,0:T(8,128)(2,1)S(1)}, bf16[32,1024]{1,0:T(8,128)(2,1)S(1)}, u32[]{:S(2)}, u32[]{:S(2)}) collective-permute-start(bf16[32,1024]{1,0:T(8,128)(2,1)S(1)} %get-tuple-element.9), channel_id=1, source_target_pairs={{0,2},{1,3},{2,0},{3,1},{4,6},{5,7},{6,4},{7,5},{8,10},{9,11},{10,... | collective-permute-start | bytes 196616 | tf_op jit(solution)/shard_map/ppermute | solution.py:392
  19.6 18.6 %collective-permute-start.11 = (bf16[32,1024]{1,0:T(8,128)(2,1)S(1)}, bf16[32,1024]{1,0:T(8,128)(2,1)S(1)}, u32[]{:S(2)}, u32[]{:S(2)}) collective-permute-start(bf16[32,1024]{1,0:T(8,128)(2,1)S(1)} %get-tuple-element.9), channel_id=1, source_target_pairs={{0,1},{1,0},{2,3},{3,2},{4,5},{5,4},{6,7},{7,6},{8,9},{9,8},{10,11... | collective-permute-start | bytes 196616 | tf_op jit(solution)/shard_map/ppermute | solution.py:392
  36.6 6.2 %collective-permute-start.8 = (bf16[2,160,256]{2,1,0:T(8,128)(2,1)S(1)}, bf16[2,160,256]{2,1,0:T(8,128)(2,1)S(1)}, u32[]{:S(2)}, u32[]{:S(2)}) collective-permute-start(bf16[2,160,256]{2,1,0:T(8,128)(2,1)S(1)} %get-tuple-element.8.refs_12_), channel_id=1, source_target_pairs={{0,1},{1,0},{2,3},{3,2},{4,5},{5,4},{6,7},{7,6},{8,9},{9,8},{10,11... | collective-permute-start | bytes 491528 | tf_op jit(solution)/shard_map/ppermute | solution.py:392
  38.2 7.7 %collective-permute-start.19 = (bf16[9,32,256]{2,1,0:T(8,128)(2,1)S(1)}, bf16[9,32,256]{2,1,0:T(8,128)(2,1)S(1)}, u32[]{:S(2)}, u32[]{:S(2)}) collective-permute-start(bf16[9,32,256]{2,1,0:T(8,128)(2,1)S(1)} %join.1.refs_16_), channel_id=1, source_target_pairs={{0,24},{4,28},{8,16},{12,20},{16,8},{20,12},{24,0},{28,4},{1,25},{... | collective-permute-start | bytes 442376 | tf_op jit(solution)/shard_map/ppermute | solution.py:377
  38.5 10.0 %collective-permute-start.17 = (bf16[9,32,256]{2,1,0:T(8,128)(2,1)S(1)}, bf16[9,32,256]{2,1,0:T(8,128)(2,1)S(1)}, u32[]{:S(2)}, u32[]{:S(2)}) collective-permute-start(bf16[9,32,256]{2,1,0:T(8,128)(2,1)S(1)} %join.1.refs_16_), channel_id=1, source_target_pairs={{0,16},{4,20},{8,24},{12,28},{16,0},{20,4},{24,8},{28,12},{1,17},{... | collective-permute-start | bytes 442376 | tf_op jit(solution)/shard_map/ppermute | solution.py:377
  39.9 9.7 %collective-permute-start.15 = (bf16[9,32,256]{2,1,0:T(8,128)(2,1)S(1)}, bf16[9,32,256]{2,1,0:T(8,128)(2,1)S(1)}, u32[]{:S(2)}, u32[]{:S(2)}) collective-permute-start(bf16[9,32,256]{2,1,0:T(8,128)(2,1)S(1)} %join.1.refs_16_), channel_id=1, source_target_pairs={{0,8},{4,12},{8,0},{12,4},{16,24},{20,28},{24,16},{28,20},{1,9},{5... | collective-permute-start | bytes 442376 | tf_op jit(solution)/shard_map/ppermute | solution.py:377
  41.7 7.8 %collective-permute-start.14 = (bf16[9,32,256]{2,1,0:T(8,128)(2,1)S(1)}, bf16[9,32,256]{2,1,0:T(8,128)(2,1)S(1)}, u32[]{:S(2)}, u32[]{:S(2)}) collective-permute-start(bf16[9,32,256]{2,1,0:T(8,128)(2,1)S(1)} %join.1.refs_16_), channel_id=1, source_target_pairs={{0,4},{4,0},{8,12},{12,8},{16,20},{20,16},{24,28},{28,24},{1,5},{5... | collective-permute-start | bytes 442376 | tf_op jit(solution)/shard_map/ppermute | solution.py:377
  42.8 9.9 %collective-permute-start.6 = (bf16[2,160,256]{2,1,0:T(8,128)(2,1)S(1)}, bf16[2,160,256]{2,1,0:T(8,128)(2,1)S(1)}, u32[]{:S(2)}, u32[]{:S(2)}) collective-permute-start(bf16[2,160,256]{2,1,0:T(8,128)(2,1)S(1)} %collective-permute-done.refs_4_), channel_id=1, source_target_pairs={{0,24},{4,28},{8,16},{12,20},{16,8},{20,12},{24,0},{28,4},{1,25},{... | collective-permute-start | bytes 491528 | tf_op jit(solution)/shard_map/ppermute | solution.py:377
  45.9 8.5 %collective-permute-start.4 = (bf16[2,160,256]{2,1,0:T(8,128)(2,1)S(1)}, bf16[2,160,256]{2,1,0:T(8,128)(2,1)S(1)}, u32[]{:S(2)}, u32[]{:S(2)}) collective-permute-start(bf16[2,160,256]{2,1,0:T(8,128)(2,1)S(1)} %collective-permute-done.refs_4_), channel_id=1, source_target_pairs={{0,16},{4,20},{8,24},{12,28},{16,0},{20,4},{24,8},{28,12},{1,17},{... | collective-permute-start | bytes 491528 | tf_op jit(solution)/shard_map/ppermute | solution.py:377
  48.4 6.9 %collective-permute-start.2 = (bf16[2,160,256]{2,1,0:T(8,128)(2,1)S(1)}, bf16[2,160,256]{2,1,0:T(8,128)(2,1)S(1)}, u32[]{:S(2)}, u32[]{:S(2)}) collective-permute-start(bf16[2,160,256]{2,1,0:T(8,128)(2,1)S(1)} %collective-permute-done.refs_4_), channel_id=1, source_target_pairs={{0,8},{4,12},{8,0},{12,4},{16,24},{20,28},{24,16},{28,20},{1,9},{5... | collective-permute-start | bytes 491528 | tf_op jit(solution)/shard_map/ppermute | solution.py:377
  49.5 5.8 %collective-permute-start.1 = (bf16[2,160,256]{2,1,0:T(8,128)(2,1)S(1)}, bf16[2,160,256]{2,1,0:T(8,128)(2,1)S(1)}, u32[]{:S(2)}, u32[]{:S(2)}) collective-permute-start(bf16[2,160,256]{2,1,0:T(8,128)(2,1)S(1)} %collective-permute-done.refs_4_), channel_id=1, source_target_pairs={{0,4},{4,0},{8,12},{12,8},{16,20},{20,16},{24,28},{28,24},{1,5},{5... | collective-permute-start | bytes 491528 | tf_op jit(solution)/shard_map/ppermute | solution.py:377
  49.5 6.3 %collective-permute-start.20 = (bf16[9,32,256]{2,1,0:T(8,128)(2,1)S(1)}, bf16[9,32,256]{2,1,0:T(8,128)(2,1)S(1)}, u32[]{:S(2)}, u32[]{:S(2)}) collective-permute-start(bf16[9,32,256]{2,1,0:T(8,128)(2,1)S(1)} %collective-permute-done.19.refs_22_), channel_id=1, source_target_pairs={{0,4},{4,0},{8,12},{12,8},{16,20},{20,16},{24,28},{28,24},{1,5},{5... | collective-permute-start | bytes 442376 | tf_op jit(solution)/shard_map/ppermute | solution.py:377
  52.6 4.6 %collective-permute-start.7 = (bf16[2,160,256]{2,1,0:T(8,128)(2,1)S(1)}, bf16[2,160,256]{2,1,0:T(8,128)(2,1)S(1)}, u32[]{:S(2)}, u32[]{:S(2)}) collective-permute-start(bf16[2,160,256]{2,1,0:T(8,128)(2,1)S(1)} %collective-permute-done.6.refs_10_), channel_id=1, source_target_pairs={{0,4},{4,0},{8,12},{12,8},{16,20},{20,16},{24,28},{28,24},{1,5},{5... | collective-permute-start | bytes 491528 | tf_op jit(solution)/shard_map/ppermute | solution.py:377
  54.4 2.8 %collective-permute-start.5 = (bf16[2,160,256]{2,1,0:T(8,128)(2,1)S(1)}, bf16[2,160,256]{2,1,0:T(8,128)(2,1)S(1)}, u32[]{:S(2)}, u32[]{:S(2)}) collective-permute-start(bf16[2,160,256]{2,1,0:T(8,128)(2,1)S(1)} %collective-permute-done.4.refs_8_), channel_id=1, source_target_pairs={{0,4},{4,0},{8,12},{12,8},{16,20},{20,16},{24,28},{28,24},{1,5},{5... | collective-permute-start | bytes 491528 | tf_op jit(solution)/shard_map/ppermute | solution.py:377
  55.3 1.9 %collective-permute-start.3 = (bf16[2,160,256]{2,1,0:T(8,128)(2,1)S(1)}, bf16[2,160,256]{2,1,0:T(8,128)(2,1)S(1)}, u32[]{:S(2)}, u32[]{:S(2)}) collective-permute-start(bf16[2,160,256]{2,1,0:T(8,128)(2,1)S(1)} %collective-permute-done.2.refs_6_), channel_id=1, source_target_pairs={{0,4},{4,0},{8,12},{12,8},{16,20},{20,16},{24,28},{28,24},{1,5},{5... | collective-permute-start | bytes 491528 | tf_op jit(solution)/shard_map/ppermute | solution.py:377
  55.3 1.6 %collective-permute-start.18 = (bf16[9,32,256]{2,1,0:T(8,128)(2,1)S(1)}, bf16[9,32,256]{2,1,0:T(8,128)(2,1)S(1)}, u32[]{:S(2)}, u32[]{:S(2)}) collective-permute-start(bf16[9,32,256]{2,1,0:T(8,128)(2,1)S(1)} %collective-permute-done.17.refs_20_), channel_id=1, source_target_pairs={{0,4},{4,0},{8,12},{12,8},{16,20},{20,16},{24,28},{28,24},{1,5},{5... | collective-permute-start | bytes 442376 | tf_op jit(solution)/shard_map/ppermute | solution.py:377
  55.8 1.4 %collective-permute-start.16 = (bf16[9,32,256]{2,1,0:T(8,128)(2,1)S(1)}, bf16[9,32,256]{2,1,0:T(8,128)(2,1)S(1)}, u32[]{:S(2)}, u32[]{:S(2)}) collective-permute-start(bf16[9,32,256]{2,1,0:T(8,128)(2,1)S(1)} %collective-permute-done.15.refs_18_), channel_id=1, source_target_pairs={{0,4},{4,0},{8,12},{12,8},{16,20},{20,16},{24,28},{28,24},{1,5},{5... | collective-permute-start | bytes 442376 | tf_op jit(solution)/shard_map/ppermute | solution.py:377
